TPU v7x, 256 devices: a whole 4x4x8 slice. The times are simulated.
256 devices in a mesh: tm: 32 (over y, x, core), height: 8 (over z).
Axes of the slice: x: 4, y: 4, z: 8, core: 2. Of those that a mesh axis runs over, the one named last changes fastest.
Arguments:
- latent: bfloat16 [64, 32, 80, 256], P('tm', 'height'), may hold values from -64 to 64, as said below
- target: bfloat16 [64, 32, 80, 256], P('tm', 'height'), may hold values from -6 to 6
- conv_weight: bfloat16 [3, 3, 3, 256, 256], replicated, may hold values from -0.078125 to 0.078125
- group_norm_gain: float32 [256], replicated, may hold values from 0.1 to 1.9
- group_norm_bias: float32 [256], replicated, may hold values from -3 to 3
Outputs:
- decoded: bfloat16 [64, 32, 80, 256], P('tm', 'height')
- grad_latent: bfloat16 [64, 32, 80, 256], P('tm', 'height')
- weight_grad: float32 [3, 3, 3, 256, 256], P(None, None, None, None, 'height')
- norm_gain_gradient: float32 [256], replicated
- bias_grad: float32 [256], replicated
Inputs may be any that keep to these rules, and one draw needn't show every extreme that they name: `latent`: finite feature values.
All inputs are finite; a program needn't handle non-finite values.
Results may differ from a plain program's by a relative error of at most 0.0015.
The roundings to bfloat16 on the way count: a program that leaves them out, or rounds other values in their place, can miss the bound.
Values may be sent and summed in bfloat16 or wider, within the bound.
A program may use at most 128 MiB of HBM per device.

v0:
```python
import jax
import jax.numpy as jnp
from jax import lax
from jax.sharding import PartitionSpec as P

NORM_GROUPS = 32


EPS = 1e-06


def shifted(value, axis, steps):
    count = lax.axis_size(axis)
    initial, last = (max(0, -steps), min(count, count - steps))
    return lax.ppermute(value, axis, [(source, source + steps) for source in range(initial, last)])


def extended(array, sides, width):
    for axis, dim in sides:
        size, length = (lax.axis_size(axis), array.shape[dim])
        up = [(i, (i + 1) % size) for i in range(size - 1)]
        down = [(j, i) for i, j in up]
        last = lax.slice_in_dim(array, length - width, length, axis=dim)
        initial = lax.slice_in_dim(array, 0, width, axis=dim)
        before = lax.ppermute(last, axis, up)
        after = lax.ppermute(initial, axis, down)
        array = jnp.concatenate([before, array, after], axis=dim)
    return array


def per_device(latent, target, conv_weight, group_norm_gain, group_norm_bias):
    frames, rows, width, channel_count = latent.shape
    channels_per_group = channel_count // NORM_GROUPS
    x32 = latent.astype(jnp.float32).reshape(-1, channel_count)
    group_view = x32.reshape(-1, NORM_GROUPS, channels_per_group)
    total = group_view.shape[0] * channels_per_group * lax.axis_size("tm") * lax.axis_size("height")
    group_average = lax.psum(jnp.sum(group_view, axis=(0, 2)), ("tm", "height")) / total
    spread = (
        lax.psum(
            jnp.sum(jnp.square(group_view - group_average[None, :, None]), axis=(0, 2)),
            ("tm", "height"),
        )
        / total
    )
    inverse_deviation = lax.rsqrt(spread + EPS)
    normalized_input = (
        (group_view - group_average[None, :, None]) * inverse_deviation[None, :, None]
    ).reshape(-1, channel_count)
    preact_values = normalized_input * group_norm_gain + group_norm_bias
    act = (
        jax.nn.silu(preact_values).astype(jnp.bfloat16).reshape(frames, rows, width, channel_count)
    )
    earlier = shifted(act, "tm", 1)
    stacked = jnp.concatenate([earlier, act], axis=0)
    apad = extended(stacked, (("height", 1),), 1)
    apad = jnp.pad(apad, ((0, 0), (0, 0), (1, 1), (0, 0)))
    conv = jnp.zeros((frames * rows * width, channel_count), jnp.float32)
    for kt in range(3):
        for kr in range(3):
            for kc in range(3):
                piece = apad[kt : kt + frames, kr : kr + rows, kc : kc + width].reshape(
                    -1, channel_count
                )
                conv = conv + jnp.dot(
                    piece, conv_weight[kt, kr, kc], preferred_element_type=jnp.float32
                )
    out = x32 + conv
    decoded = out.astype(jnp.bfloat16).reshape(frames, rows, width, channel_count)
    output_gradient = out - target.astype(jnp.float32).reshape(-1, channel_count)
    grad_half = output_gradient.astype(jnp.bfloat16)
    grad_block = grad_half.reshape(frames, rows, width, channel_count)
    later = shifted(grad_block, "tm", -1)
    gstack = jnp.concatenate([grad_block, later], axis=0)
    gpad = extended(gstack, (("height", 1),), 1)
    gpad = jnp.pad(gpad, ((0, 0), (0, 0), (1, 1), (0, 0)))
    back = jnp.zeros((frames * rows * width, channel_count), jnp.float32)
    taps = []
    for kt in range(3):
        for kr in range(3):
            for kc in range(3):
                piece = apad[kt : kt + frames, kr : kr + rows, kc : kc + width].reshape(
                    -1, channel_count
                )
                taps.append(
                    lax.dot_general(
                        piece,
                        grad_half,
                        (((0,), (0,)), ((), ())),
                        preferred_element_type=jnp.float32,
                    )
                )
                gpiece = gpad[
                    2 - kt : 2 - kt + frames, 2 - kr : 2 - kr + rows, 2 - kc : 2 - kc + width
                ].reshape(-1, channel_count)
                back = back + jnp.dot(
                    gpiece, conv_weight[kt, kr, kc].T, preferred_element_type=jnp.float32
                )
    partial_w = jnp.stack(taps).reshape(3, 3, 3, channel_count, channel_count)
    share = channel_count // lax.axis_size("height")
    summed_w = lax.psum(partial_w, ("tm", "height"))
    weight_grad = lax.dynamic_slice_in_dim(summed_w, lax.axis_index("height") * share, share, 4)
    sig = jax.nn.sigmoid(preact_values)
    preact_gradient = back * sig * (1.0 + preact_values * (1.0 - sig))
    normalized_gradient = preact_gradient * group_norm_gain
    norm_gain_gradient, bias_grad, first_sum, second_sum = lax.psum(
        (
            jnp.sum(preact_gradient * normalized_input, axis=0),
            jnp.sum(preact_gradient, axis=0),
            jnp.sum(normalized_gradient.reshape(-1, NORM_GROUPS, channels_per_group), axis=(0, 2)),
            jnp.sum(
                (normalized_gradient * normalized_input).reshape(
                    -1, NORM_GROUPS, channels_per_group
                ),
                axis=(0, 2),
            ),
        ),
        ("tm", "height"),
    )
    first_moment = jnp.repeat(first_sum / total, channels_per_group)
    second_moment = jnp.repeat(second_sum / total, channels_per_group)
    channel_inverse_deviation = jnp.repeat(inverse_deviation, channels_per_group)
    input_gradient = output_gradient + channel_inverse_deviation * (
        normalized_gradient - first_moment - normalized_input * second_moment
    )
    grad_latent = input_gradient.astype(jnp.bfloat16).reshape(frames, rows, width, channel_count)
    return (decoded, grad_latent, weight_grad, norm_gain_gradient, bias_grad)


def solution(mesh):
    in_specs = (P("tm", "height", None, None), P("tm", "height", None, None), P(), P(), P())
    out_specs = (
        P("tm", "height", None, None),
        P("tm", "height", None, None),
        P(None, None, None, None, "height"),
        P(),
        P(),
    )
    return jax.shard_map(
        per_device, mesh=mesh, in_specs=in_specs, out_specs=out_specs, check_vma=False
    )
```

profile of v0, /device:TPU:1, one launch (start us, length us, event | category | flops | bytes accessed | tf_op | source)
XLA Modules:
  0.0 525.3 jit_solution(2615126886422578941)
XLA Ops:
  7.2 1.1 convert_reduce_fusion
  8.5 81.4 %psum.49 = f32[32]{0:T(128)S(1)} all-reduce(f32[32]{0:T(128)S(1)} %reduce_sum.67), channel_id=1, replica_groups=mesh['tm'=32,'height'=8] {'tm','height'}, use_global_device_ids=true, to_apply=%region_2.0 | all-reduce | flops 32 | bytes 256 | tf_op jit(solution)/shard_map/psum | solution.py:37
  90.1 1.1 multiply_reduce_fusion.2
  91.4 72.4 %psum.50 = f32[32]{0:T(128)S(1)} all-reduce(f32[32]{0:T(128)S(1)} %reduce_sum.73), channel_id=1, replica_groups=mesh['tm'=32,'height'=8] {'tm','height'}, use_global_device_ids=true, to_apply=%region_5.6 | all-reduce | flops 32 | bytes 256 | tf_op jit(solution)/shard_map/psum | solution.py:39
  163.9 1.2 multiply_convert_fusion
  165.2 2.8 collective-permute-start
  168.0 4.0 collective-permute-done
  172.1 3.7 collective-permute-start.1
  175.8 1.5 collective-permute-start.2
  177.2 1.0 fusion.38
  178.3 3.5 collective-permute-done.2
  183.2 1.2 copy-done
  191.6 1.0 fusion.34
  195.6 1.0 fusion.30
  198.6 1.0 fusion.27
  199.7 1.0 fusion.26
  201.7 1.0 fusion.24
  202.7 1.0 fusion.23
  204.8 1.0 fusion.21
  205.8 1.0 fusion.20
  211.8 1.0 fusion.14
  214.9 1.0 fusion.11
  215.9 1.9 collective-permute-start.3
  219.8 6.9 %collective-permute-done.3 = bf16[2,4,80,256]{3,2,1,0:T(8,128)(2,1)S(1)} collective-permute-done((bf16[2,4,80,256]{3,2,1,0:T(8,128)(2,1)S(1)}, bf16[2,4,80,256]{3,2,1,0:T(8,128)(2,1)S(1)}, u32[]{:S(2)}, u32[]{:S(2)}) %collective-permute-start.3) | collective-permute-done | bytes 327712 | tf_op jit(solution)/shard_map/ppermute | solution.py:15
  226.8 1.4 collective-permute-start.4
  228.2 1.5 collective-permute-start.5
  230.7 8.1 %copy.11 = f32[3,3,3,256,256]{3,4,2,1,0:T(8,128)} copy(f32[3,3,3,256,256]{4,3,2,1,0:T(8,128)} %bitcast.112) | data formatting | bytes 14155776 | tf_op jit(solution)/shard_map/reshape | solution.py:98
  240.5 1.2 copy-done.1
  250.3 80.0 %all-reduce.2 = (f32[32]{0:T(128)S(1)}, f32[32]{0:T(128)S(1)}, f32[256]{0:T(256)}, f32[256]{0:T(256)}) all-reduce(f32[32]{0:T(128)S(1)} %reduce_sum.93, f32[32]{0:T(128)S(1)} %reduce_sum.90, f32[256]{0:T(256)S(1)} %get-tuple-element.5, f32[256]{0:T(256)S(1)} %get-tuple-element.8), channel_id=1, replica_groups=mesh['tm'=32,'height'=8] {'tm','height'}, use_global_device_ids=true, to_apply=%region_11.12 | all-reduce | flops 576 | bytes 4608 | tf_op jit(solution)/shard_map/psum | solution.py:105
  330.6 1.1 add_convert_fusion
  331.7 184.6 %all-reduce.5.cloned.1.call-done = f32[3,3,3,256,256]{3,4,2,1,0:T(8,128)} async-done(((f32[3,3,3,256,256]{3,4,2,1,0:T(8,128)}), f32[3,3,3,256,256]{3,4,2,1,0:T(8,128)}) %all-reduce.5.cloned.1.call-update) | async-done | bytes 7077904 | tf_op jit(solution)/shard_map/psum | solution.py:100
  516.3 2.2 constant_dynamic-slice_fusion
  (119 shorter events, 36.6 us)
Async XLA Ops:
  7.2 509.1 %all-reduce.5.cloned.1.call-start = ((), (), s32[]{:S(2)}) async-start(), calls=%async_computation | async-start | bytes 14155776 | tf_op jit(solution)/shard_map/psum | solution.py:100
  165.2 6.8 %collective-permute-start = (bf16[2,4,80,256]{3,2,1,0:T(8,128)(2,1)S(1)}, bf16[2,4,80,256]{3,2,1,0:T(8,128)(2,1)S(1)}, u32[]{:S(2)}, u32[]{:S(2)}) collective-permute-start(bf16[2,4,80,256]{3,2,1,0:T(8,128)(2,1)S(1)} %multiply_convert_fusion), channel_id=1, source_target_pairs={{0,8},{8,16},{16,24},{24,32},{32,40},{40,48},{48,56},{56,64},{64,7... | collective-permute-start | bytes 983048 | tf_op jit(solution)/shard_map/ppermute | solution.py:15
  172.1 6.3 %collective-permute-start.1 = (bf16[4,1,80,256]{3,2,1,0:T(8,128)(2,1)S(1)}, bf16[4,1,80,256]{3,2,1,0:T(8,128)(2,1)S(1)}, u32[]{:S(2)}, u32[]{:S(2)}) collective-permute-start(bf16[4,1,80,256]{3,2,1,0:T(8,128)(2,1)S(1)} %get-tuple-element.69), channel_id=1, source_target_pairs={{0,1},{1,2},{2,3},{3,4},{4,5},{5,6},{6,7},{8,9},{9,10},{10,11},{11... | collective-permute-start | bytes 491528 | tf_op jit(solution)/shard_map/ppermute | solution.py:25
  175.8 6.1 %collective-permute-start.2 = (bf16[4,1,80,256]{3,2,1,0:T(8,128)(2,1)S(1)}, bf16[4,1,80,256]{3,2,1,0:T(8,128)(2,1)S(1)}, u32[]{:S(2)}, u32[]{:S(2)}) collective-permute-start(bf16[4,1,80,256]{3,2,1,0:T(8,128)(2,1)S(1)} %get-tuple-element.70), channel_id=1, source_target_pairs={{1,0},{2,1},{3,2},{4,3},{5,4},{6,5},{7,6},{9,8},{10,9},{11,10},{12... | collective-permute-start | bytes 491528 | tf_op jit(solution)/shard_map/ppermute | solution.py:26
  182.4 2.0 copy-start
  190.2 1.0 copy-start.2
  190.2 1.1 copy-start.3
  215.9 10.9 %collective-permute-start.3 = (bf16[2,4,80,256]{3,2,1,0:T(8,128)(2,1)S(1)}, bf16[2,4,80,256]{3,2,1,0:T(8,128)(2,1)S(1)}, u32[]{:S(2)}, u32[]{:S(2)}) collective-permute-start(bf16[2,4,80,256]{3,2,1,0:T(8,128)(2,1)S(1)} %bitcast.427), channel_id=1, source_target_pairs={{8,0},{16,8},{24,16},{32,24},{40,32},{48,40},{56,48},{64,56},{72,6... | collective-permute-start | bytes 983048 | tf_op jit(solution)/shard_map/ppermute | solution.py:15
  226.8 12.1 %collective-permute-start.4 = (bf16[4,1,80,256]{3,2,1,0:T(8,128)(2,1)S(1)}, bf16[4,1,80,256]{3,2,1,0:T(8,128)(2,1)S(1)}, u32[]{:S(2)}, u32[]{:S(2)}) collective-permute-start(bf16[4,1,80,256]{3,2,1,0:T(8,128)(2,1)S(1)} %get-tuple-element.65), channel_id=1, source_target_pairs={{0,1},{1,2},{2,3},{3,4},{4,5},{5,6},{6,7},{8,9},{9,10},{10,11},{11... | collective-permute-start | bytes 491528 | tf_op jit(solution)/shard_map/ppermute | solution.py:25
  228.2 10.7 %collective-permute-start.5 = (bf16[4,1,80,256]{3,2,1,0:T(8,128)(2,1)S(1)}, bf16[4,1,80,256]{3,2,1,0:T(8,128)(2,1)S(1)}, u32[]{:S(2)}, u32[]{:S(2)}) collective-permute-start(bf16[4,1,80,256]{3,2,1,0:T(8,128)(2,1)S(1)} %get-tuple-element.66), channel_id=1, source_target_pairs={{1,0},{2,1},{3,2},{4,3},{5,4},{6,5},{7,6},{9,8},{10,9},{11,10},{12... | collective-permute-start | bytes 491528 | tf_op jit(solution)/shard_map/ppermute | solution.py:26
  239.7 2.0 copy-start.1
  248.1 1.2 copy-start.4
  248.1 1.2 copy-start.5
Sparse Core Ops, SparseCore 0:
  239.0 277.2 all-reduce.4
where the time goes:
time: 527 us; the launch traced here: 525 us
  blocking collectives  234 us (44%)
  waiting for transfers between devices  199 us (38%)
  matrix products  41.8 us (8%)
  local copies, waits for them, and re-layouts  15.6 us (3%)
  between operations  14.7 us (3%)
  starting transfers between devices  12.9 us (2%)
  other arithmetic  7.53 us (1%)
    psum x1, waiting for transfers between devices, per_device(): summed_w = lax.psum(partial_w, ('tm', 'height'))  185 us
    psum x1, blocking collectives, per_device(): lax.psum(jnp.sum(group_view, axis=(0, 2)), ('tm', 'height')) / total  81.4 us
    psum x1, blocking collectives, per_device(): lax.psum((jnp.sum(preact_gradient * normalized_input, axis=0), jnp.sum(pr...  80 us
    psum x1, blocking collectives, per_device(): lax.psum(jnp.sum(jnp.square(group_view - group_average[None, :, None]), a...  72.4 us
    dot_general x27, matrix products, per_device(): lax.dot_general(piece, grad_half, (((0,), (0,)), ((), ())), preferred_ele...  27.3 us
    ppermute x2, waiting for transfers between devices, shifted(): lax.ppermute(value, axis, [(source, source + steps) for source in range(i...  10.9 us
  transfers between devices with their start and end apart: 7, of which 4 were waited for; matrix products, arithmetic and copies ran while one was open for 4% of the time, Pallas kernels for 0%

commit v1 on v0

v1 whole, which is shorter than its diff:
```python
import functools

import jax
import jax.numpy as jnp
from jax import lax
from jax.experimental import pallas as pl
from jax.experimental.pallas import tpu as pltpu
from jax.sharding import PartitionSpec as P

NORM_GROUPS = 32
EPS = 1e-06
MESH = pl.DeviceIdType.MESH
F32 = jnp.float32
BF16 = jnp.bfloat16
UA = 5
UB = 4


def group_sum(v):
    lane = lax.broadcasted_iota(jnp.int32, v.shape, 1)
    width = v.shape[1]
    for k in (1, 2, 4):
        other = jnp.where(
            lax.rem(lax.div(lane, k), 2) == 1,
            pltpu.roll(v, k, 1),
            pltpu.roll(v, width - k, 1),
        )
        v = v + other
    return v


def pack(a, b):
    half = a.shape[1] // 2
    return jnp.concatenate(
        [a[:, :half], a[:, half:], b[:, :half], b[:, half:], jnp.zeros((4, half), F32)], axis=0
    )


def unpack(v):
    a = jnp.concatenate([v[0:1], v[1:2]], axis=1)
    b = jnp.concatenate([v[2:3], v[3:4]], axis=1)
    return a, b


def kernel(
    nx, ny, nz, cells,
    latent, target_hbm, w_hbm, gain_ref, bias_ref,
    decoded, grad_latent, wgrad, ngrad, bgrad,
    L, A, G, graw, g32, acc, W, WT, target, gta, gtb,
    DA, DB, RCA, RCB,
    axp, axm, axf, azp, azm, azf, bzp, bzm, bzf, bxp, bxm, bxf,
    YB, XG, AR,
    in_sem, lat_s, lat_r, gh_s, gh_r, ar_s, ar_r, co_s, co_r,
    ring_s, ring_r, y_s, y_r, xg_s, xg_r, cg_s, cg_r,
):
    t = lax.axis_index("tm")
    z = lax.axis_index("height")
    nt = 2 * nx * ny
    core = lax.rem(t, 2)
    x = lax.rem(lax.div(t, 2), nx)
    y = lax.div(t, 2 * nx)
    frames, rows, width, ch = latent.shape

    def at(yy, xx, cc):
        return (yy * nx + xx) * 2 + cc

    def remote(src, dst, ss, rs, tt, zz):
        return pltpu.make_async_remote_copy(
            src_ref=src, dst_ref=dst, send_sem=ss, recv_sem=rs,
            device_id=(tt, zz), device_id_type=MESH,
        )

    up_t, dn_t = lax.rem(t + 1, nt), lax.rem(t + nt - 1, nt)
    up_z, dn_z = lax.rem(z + 1, nz), lax.rem(z + nz - 1, nz)
    up_x, dn_x = lax.rem(x + 1, nx), lax.rem(x + nx - 1, nx)

    n1, n2 = 2 * nz, nx * ny
    me1, me2 = core * nz + z, y * nx + x

    def peer1(k):
        p = lax.rem(me1 + k, n1)
        return at(y, x, lax.div(p, nz)), lax.rem(p, nz)

    def peer2(k):
        p = lax.rem(me2 + k, n2)
        return p * 2 + core, z

    barrier = pltpu.get_barrier_semaphore()

    def greet(tt, zz):
        pl.semaphore_signal(barrier, inc=1, device_id=(tt, zz), device_id_type=MESH)

    def greet1(k, c):
        greet(*peer1(k))
        return c

    def greet2(k, c):
        greet(*peer2(k))
        return c

    lax.fori_loop(1, n1, greet1, 0)
    lax.fori_loop(1, n2, greet2, 0)
    for tt in (up_t, dn_t):
        for zz in (dn_z, z, up_z):
            greet(tt, zz)

    weights_in = pltpu.make_async_copy(w_hbm, W, in_sem.at[0])
    target_in = pltpu.make_async_copy(target_hbm, target, in_sem.at[1])
    weights_in.start()
    target_in.start()

    def sum_rows(i, total):
        v = latent[lax.div(i, rows), lax.rem(i, rows)].astype(F32)
        return total + jnp.sum(v.reshape(width // 8, 8, ch), axis=0)

    count = frames * rows * width * 8
    total = lax.fori_loop(0, frames * rows, sum_rows, jnp.zeros((8, ch), F32))
    mean_l = group_sum(jnp.sum(total, axis=0, keepdims=True)) / count

    def sum_squares(i, total):
        v = latent[lax.div(i, rows), lax.rem(i, rows)].astype(F32) - mean_l
        return total + jnp.sum((v * v).reshape(width // 8, 8, ch), axis=0)

    total = lax.fori_loop(0, frames * rows, sum_squares, jnp.zeros((8, ch), F32))
    sq_l = group_sum(jnp.sum(total, axis=0, keepdims=True))

    pl.semaphore_wait(barrier, (n1 - 1) + (n2 - 1) + 6)

    def spread_out(stage, value):
        me, n, peer = (me1, n1, peer1) if stage % 2 == 0 else (me2, n2, peer2)
        slots = AR.at[stage]
        AR[stage, me] = value

        def send(k, c):
            tt, zz = peer(k)
            remote(slots.at[me], slots.at[me], ar_s.at[stage, k], ar_r.at[stage, k], tt, zz).start()
            return c

        lax.fori_loop(1, n, send, 0)

    def gather_in(stage):
        me, n, peer = (me1, n1, peer1) if stage % 2 == 0 else (me2, n2, peer2)
        slots = AR.at[stage]

        def arrive(k, c):
            tt, zz = peer(k)
            remote(slots.at[me], slots.at[me], ar_s.at[stage, k], ar_r.at[stage, k], tt, zz).wait()
            return c

        lax.fori_loop(1, n, arrive, 0)
        return n

    def plain_total(stage, n):
        total = AR[stage, 0]
        for k in range(1, n):
            total = total + AR[stage, k]
        return total

    def moments(stage, n, members):
        mean = plain_total(stage, n) / n
        row = lax.broadcasted_iota(jnp.int32, mean.shape, 0)
        mean = mean[0:2]
        sq = jnp.zeros_like(mean)
        for k in range(n):
            d = AR[stage, k, 0:2] - mean
            sq = sq + (AR[stage, k, 2:4] + (d * d) * members)
        del row
        return jnp.concatenate([mean, sq, jnp.zeros((4, mean.shape[1]), F32)], axis=0)

    spread_out(0, pack(mean_l, sq_l))

    def halo(block, buf, first, other, tt, ss, rs):
        edge0, edge1 = block.at[:, 0], block.at[:, rows - 1]
        mine, theirs = pl.ds(first, frames), pl.ds(other, frames)
        return [
            remote(block, buf.at[theirs, pl.ds(1, rows)], ss.at[0], rs.at[0], tt, z),
            remote(edge1, buf.at[mine, 0], ss.at[1], rs.at[1], t, up_z),
            remote(edge0, buf.at[mine, rows + 1], ss.at[2], rs.at[2], t, dn_z),
            remote(edge1, buf.at[theirs, 0], ss.at[3], rs.at[3], tt, up_z),
            remote(edge0, buf.at[theirs, rows + 1], ss.at[4], rs.at[4], tt, dn_z),
        ]

    lat_halo = halo(latent, L, frames, 0, up_t, lat_s, lat_r)
    for c in lat_halo:
        c.start()
    for f in range(frames):
        for r in range(rows):
            L[frames + f, 1 + r] = latent[f, r]

    weights_in.wait()

    def flip(u, c):
        for kc in range(3):
            WT[8 - u, (2 - kc) * ch : (3 - kc) * ch, :] = W[u, kc * ch : (kc + 1) * ch, :].T
        return c

    n = gather_in(0)
    level = moments(0, n, count)
    spread_out(1, level)
    lax.fori_loop(0, 9, flip, 0)
    n = gather_in(1)
    mean, sq = unpack(moments(1, n, count * n1))
    everything = count * n1 * n2
    rstd = lax.rsqrt(sq / everything + EPS)
    gain, bias = gain_ref[...], bias_ref[...]
    scale = rstd * gain

    for c in lat_halo:
        c.wait()

    col = lax.broadcasted_iota(jnp.int32, (width, ch), 0)

    def store_shifts(buf, f, r, v):
        buf[f, r, :, 0:ch] = jnp.where(col == 0, 0.0, pltpu.roll(v, 1, 0)).astype(BF16)
        buf[f, r, :, ch : 2 * ch] = v.astype(BF16)
        buf[f, r, :, 2 * ch : 3 * ch] = jnp.where(
            col == width - 1, 0.0, pltpu.roll(v, width - 1, 0)
        ).astype(BF16)

    def inside(f, r, lone, edge):
        top = jnp.logical_or(r > 0, z > 0)
        low = jnp.logical_or(r < rows + 1, z < nz - 1)
        return jnp.logical_and(jnp.logical_or(lone, edge), jnp.logical_and(top, low))

    def activate(i, c):
        f, r = lax.div(i, rows + 2), lax.rem(i, rows + 2)
        zz = (L[f, r].astype(F32) - mean) * scale + bias
        v = zz / (1.0 + jnp.exp(-zz))
        keep = inside(f, r, f >= frames, t > 0)
        store_shifts(A, f, r, jnp.where(keep, v, 0.0))
        return c

    lax.fori_loop(0, 2 * frames * (rows + 2), activate, 0)

    size = frames * rows * width

    def piece(buf, u):
        kt, kr = lax.div(u, 3), lax.rem(u, 3)
        return buf[pl.ds(kt, frames), pl.ds(kr, rows)].reshape(size, 3 * ch)

    def conv(buf, w):
        acc[...] = jnp.dot(piece(buf, 0), w[0], preferred_element_type=F32)

        def tap(u, c):
            acc[...] += jnp.dot(piece(buf, u), w[u], preferred_element_type=F32)
            return c

        lax.fori_loop(1, 9, tap, 0)

    conv(A, W)
    target_in.wait()

    def finish(i, c):
        f, r = lax.div(i, rows), lax.rem(i, rows)
        at_row = pl.ds(pl.multiple_of(i * width, 16), width)
        out = latent[f, r].astype(F32) + acc[at_row, :]
        decoded[f, r] = out.astype(BF16)
        g = out - target[f, r].astype(F32)
        g32[at_row, :] = g
        graw[f, 1 + r] = g.astype(BF16)
        return c

    lax.fori_loop(0, frames * rows, finish, 0)

    own = graw.at[pl.ds(0, frames), pl.ds(1, rows)]
    g_halo = halo(own, graw, 0, frames, dn_t, gh_s, gh_r)
    for c in g_halo:
        c.start()

    per = ch // (nx * nz)
    for b in range(ch // 128):
        for s in range(size // 128):
            gtb[b * 128 : (b + 1) * 128, s * 128 : (s + 1) * 128] = (
                g32[s * 128 : (s + 1) * 128, b * 128 : (b + 1) * 128].T
            )
    for zz in range(nz):
        for xx in range(nx):
            gta[(xx * nz + zz) * per : (xx * nz + zz + 1) * per] = (
                gtb[(zz * nx + xx) * per : (zz * nx + xx + 1) * per]
            )

    other = 1 - core

    def to_sibling_a(u):
        return remote(DA.at[other, u], RCA.at[u], co_s.at[u], co_r.at[u], at(y, x, other), z)

    def to_sibling_b(u):
        return remote(
            DB.at[other, u], RCB.at[u], co_s.at[UA + u], co_r.at[UA + u], at(y, x, other), z
        )

    half = ch // 2

    def kernel_term(gt, D, unit, u):
        res = jnp.dot(gt[...].astype(BF16), piece(A, unit), preferred_element_type=F32)
        d = D.shape
        for kc in range(3):
            for h in range(2):
                lo = kc * ch + h * half
                D[h, u, :, :, kc] = res[:, lo : lo + half].reshape(d[2], d[3], per, half)

    def term_a(u, c):
        kernel_term(gta, DA, u, u)
        to_sibling_a(u).start()
        return c

    def term_b(u, c):
        kernel_term(gtb, DB, UA + u, u)
        to_sibling_b(u).start()
        return c

    lax.fori_loop(0, UB, term_b, 0)
    lax.fori_loop(0, UA, term_a, 0)

    class Ring:
        def __init__(self, n, me, up, down, chunk, cut, first, second, full, unit, step0):
            self.n, self.me, self.up, self.down = n, me, up, down
            self.chunk, self.cut = chunk, cut
            self.first, self.second, self.full = first, second, full
            self.unit, self.step0 = unit, step0
            self.steps = n // 2

        def sends(self, u, s):
            n, me, k, i = self.n, self.me, self.unit(u), self.step0 + s
            sems = [(ring_s.at[k, i, d], ring_r.at[k, i, d]) for d in range(2)]
            if s == 0:
                c = self.chunk(u, lax.rem(me + n // 2, n))
                size_ = c.shape[0]
                src = [c.at[pl.ds(0, self.cut)], c.at[pl.ds(self.cut, size_ - self.cut)]]
                dst = [self.first.at[u], self.second.at[u]]
            else:
                src = [
                    self.chunk(u, lax.rem(me + n // 2 - s, n)),
                    self.chunk(u, lax.rem(me + n - n // 2 + s, n)),
                ]
                dst = [self.full.at[u, s - 1, 0], self.full.at[u, s - 1, 1]]
            return [
                remote(src[0], dst[0], *sems[0], *self.up),
                remote(src[1], dst[1], *sems[1], *self.down),
            ]

        def send(self, u, s):
            for c in self.sends(u, s):
                c.start()

        def receive(self, u, s):
            n, me = self.n, self.me
            for c in self.sends(u, s):
                c.wait_recv()
            left = self.chunk(u, lax.rem(me + n - 1 + n // 2 - s, n))
            right = self.chunk(u, lax.rem(me + n + 1 - n // 2 + s, n))
            if s == 0:
                size_ = left.shape[0]
                head, tail = pl.ds(0, self.cut), pl.ds(self.cut, size_ - self.cut)
                left[head] = left[head] + self.first[u]
                right[tail] = right[tail] + self.second[u]
            else:
                left[...] = left[...] + self.full[u, s - 1, 0]
                right[...] = right[...] + self.full[u, s - 1, 1]

        def sent(self, u, s):
            for c in self.sends(u, s):
                c.wait_send()

    x_up, x_down = (at(y, up_x, core), z), (at(y, dn_x, core), z)
    z_up, z_down = (t, up_z), (t, dn_z)
    sx, sz = nx // 2, nz // 2
    a_unit = lambda u: u
    b_unit = lambda u: UA + u
    ring_ax = Ring(
        nx, x, x_up, x_down, lambda u, c: DA.at[core, u, c], nz // 2, axp, axm, axf, a_unit, 0
    )
    ring_az = Ring(
        nz, z, z_up, z_down, lambda u, c: DA.at[core, u, x, c], 2, azp, azm, azf, a_unit, sx
    )
    ring_bz = Ring(
        nz, z, z_up, z_down, lambda u, c: DB.at[core, u, c], nx // 2, bzp, bzm, bzf, b_unit, 0
    )
    ring_bx = Ring(
        nx, x, x_up, x_down, lambda u, c: DB.at[core, u, z, c], 2, bxp, bxm, bxf, b_unit, sz
    )
    plan_a = [(ring_ax, s) for s in range(sx)] + [(ring_az, s) for s in range(sz)]
    plan_b = [(ring_bz, s) for s in range(sz)] + [(ring_bx, s) for s in range(sx)]

    def first_a(u, c):
        to_sibling_a(u).wait_recv()
        DA[core, u] = DA[core, u] + RCA[u]
        plan_a[0][0].send(u, 0)
        return c

    def first_b(u, c):
        to_sibling_b(u).wait_recv()
        DB[core, u] = DB[core, u] + RCB[u]
        plan_b[0][0].send(u, 0)
        return c

    lax.fori_loop(0, UB, first_b, 0)
    lax.fori_loop(0, UA, first_a, 0)

    def wave(w):
        def go(plan, u):
            ring, s = plan[w]
            ring.receive(u, s)
            if w + 1 < len(plan):
                ring, s = plan[w + 1]
                ring.send(u, s)

        def go_a(u, c):
            go(plan_a, u)
            return c

        def go_b(u, c):
            go(plan_b, u)
            return c

        lax.fori_loop(0, UB, go_b, 0)
        lax.fori_loop(0, UA, go_a, 0)

    for c in g_halo:
        c.wait()

    def shift_gradient(i, c):
        f, r = lax.div(i, rows + 2), lax.rem(i, rows + 2)
        keep = inside(f, r, f < frames, t < nt - 1)
        store_shifts(G, f, r, jnp.where(keep, graw[f, r].astype(F32), 0.0))
        return c

    lax.fori_loop(0, 2 * frames * (rows + 2), shift_gradient, 0)
    wave(0)
    conv(G, WT)

    def through_norm(i, carry):
        s0, s1 = carry
        f, r = lax.div(i, rows), lax.rem(i, rows)
        at_row = pl.ds(pl.multiple_of(i * width, 16), width)
        d = latent[f, r].astype(F32) - mean
        zz = d * scale + bias
        sig = 1.0 / (1.0 + jnp.exp(-zz))
        gz = acc[at_row, :] * sig * (1.0 + zz * (1.0 - sig))
        acc[at_row, :] = gz
        xhat = d * rstd
        s0 = s0 + jnp.sum(gz.reshape(width // 8, 8, ch), axis=0)
        s1 = s1 + jnp.sum((gz * xhat).reshape(width // 8, 8, ch), axis=0)
        return s0, s1

    zero = jnp.zeros((8, ch), F32)
    s0, s1 = lax.fori_loop(0, frames * rows, through_norm, (zero, zero))
    spread_out(2, pack(jnp.sum(s0, axis=0, keepdims=True), jnp.sum(s1, axis=0, keepdims=True)))
    last = len(plan_a)
    if last > 1:
        wave(1)
    n = gather_in(2)
    spread_out(3, plain_total(2, n))
    if last > 2:
        wave(2)
    n = gather_in(3)
    s0, s1 = unpack(plain_total(3, n))
    bgrad[...] = s0
    ngrad[...] = s1
    m1 = group_sum(s0 * gain) / everything
    m2 = group_sum(s1 * gain) / everything

    def to_input(i, c):
        f, r = lax.div(i, rows), lax.rem(i, rows)
        at_row = pl.ds(pl.multiple_of(i * width, 16), width)
        xhat = (latent[f, r].astype(F32) - mean) * rstd
        gx = acc[at_row, :] * gain
        grad_latent[f, r] = (g32[at_row, :] + rstd * (gx - m1 - xhat * m2)).astype(BF16)
        return c

    lax.fori_loop(0, frames * rows, to_input, 0)
    for w in range(3, last):
        wave(w)

    for u in range(UA):
        YB[y, u] = DA[core, u, x, z]
    for u in range(UB):
        YB[y, UA + u] = DB[core, u, z, x]

    def y_copy(k):
        yy = lax.rem(y + k, ny)
        return remote(YB.at[y], YB.at[y], y_s.at[k], y_r.at[k], at(yy, x, core), z)

    for k in range(1, ny):
        y_copy(k).start()
    for k in range(1, ny):
        y_copy(k).wait()
    total = YB[0]
    for k in range(1, ny):
        total = total + YB[k]
    XG[x, core] = total

    def to_x(src, units, up, i):
        first, many = units
        ref = XG.at[src, core, pl.ds(first, many)]
        return remote(ref, ref, xg_s.at[i], xg_r.at[i], at(y, up_x if up else dn_x, core), z)

    def to_core(src, i):
        ref = XG.at[src, core]
        return remote(ref, ref, cg_s.at[i], cg_r.at[i], at(y, x, other), z)

    whole = (0, UA + UB)
    step1 = [to_x(x, whole, True, 0), to_x(x, whole, False, 1)]
    cores = [to_core(x, 0), to_core(dn_x, 1), to_core(up_x, 2), to_core(lax.rem(x + 2, nx), 3)]
    for c in step1 + cores[:1]:
        c.start()
    step1[0].wait_recv()
    step2 = [to_x(dn_x, (0, UA), True, 2), to_x(up_x, (UA, UB), False, 3)]
    step2[0].start()
    cores[1].start()
    step1[1].wait_recv()
    step2[1].start()
    cores[2].start()
    for c in step2:
        c.wait_recv()
    cores[3].start()
    for c in cores:
        c.wait_recv()
    for xx in range(nx):
        for cc in range(2):
            rows_ = slice(xx * per, (xx + 1) * per)
            wgrad[:, :, rows_, cc * half : (cc + 1) * half] = XG[xx, cc]

    for c in step1 + step2 + cores:
        c.wait_send()

    def drain_a(u, c):
        to_sibling_a(u).wait_send()
        for ring, s in plan_a:
            ring.sent(u, s)
        return c

    def drain_b(u, c):
        to_sibling_b(u).wait_send()
        for ring, s in plan_b:
            ring.sent(u, s)
        return c

    lax.fori_loop(0, UA, drain_a, 0)
    lax.fori_loop(0, UB, drain_b, 0)


def per_device(nx, ny, nz, latent, target, conv_weight, gain, bias):
    frames, rows, width, ch = latent.shape
    size = frames * rows * width
    per, half = ch // (nx * nz), ch // 2
    sx, sz = nx // 2, nz // 2
    units = UA + UB
    tile = (3, per, half)
    V, D = pltpu.VMEM, pltpu.SemaphoreType.DMA
    big = (2 * frames, rows + 2, width, 3 * ch)
    scratch = [
        V((2 * frames, rows + 2, width, ch), BF16),
        V(big, BF16),
        V(big, BF16),
        V((2 * frames, rows + 2, width, ch), BF16),
        V((size, ch), F32),
        V((size, ch), F32),
        V((9, 3 * ch, ch), BF16),
        V((9, 3 * ch, ch), BF16),
        V((frames, rows, width, ch), BF16),
        V((ch, size), F32),
        V((ch, size), F32),
        V((2, UA, nx, nz) + tile, F32),
        V((2, UB, nz, nx) + tile, F32),
        V((UA, nx, nz) + tile, F32),
        V((UB, nz, nx) + tile, F32),
        V((UA, nz // 2) + tile, F32),
        V((UA, nz - nz // 2) + tile, F32),
        V((UA, max(sx - 1, 1), 2, nz) + tile, F32),
        V((UA, 2, per, half), F32),
        V((UA, 1, per, half), F32),
        V((UA, max(sz - 1, 1), 2) + tile, F32),
        V((UB, nx // 2) + tile, F32),
        V((UB, nx - nx // 2) + tile, F32),
        V((UB, max(sz - 1, 1), 2, nx) + tile, F32),
        V((UB, 2, per, half), F32),
        V((UB, 1, per, half), F32),
        V((UB, max(sx - 1, 1), 2) + tile, F32),
        V((ny, units) + tile, F32),
        V((nx, 2, units) + tile, F32),
        V((4, max(2 * nz, nx * ny), 8, half), F32),
        D((2,)),
        D((5,)), D((5,)), D((5,)), D((5,)),
        D((4, max(2 * nz, nx * ny))), D((4, max(2 * nz, nx * ny))),
        D((units,)), D((units,)),
        D((units, sx + sz, 2)), D((units, sx + sz, 2)),
        D((ny,)), D((ny,)),
        D((4,)), D((4,)), D((4,)), D((4,)),
    ]
    vm = pl.BlockSpec(memory_space=pltpu.VMEM)
    anywhere = pl.BlockSpec(memory_space=pl.ANY)
    outs = [
        jax.ShapeDtypeStruct(latent.shape, BF16),
        jax.ShapeDtypeStruct(latent.shape, BF16),
        jax.ShapeDtypeStruct((9, 3, ch // nz, ch), F32),
        jax.ShapeDtypeStruct((1, ch), F32),
        jax.ShapeDtypeStruct((1, ch), F32),
    ]
    decoded, grad_latent, wgrad, ngrad, bgrad = pl.pallas_call(
        functools.partial(kernel, nx, ny, nz, size),
        out_shape=outs,
        in_specs=[vm, anywhere, anywhere, vm, vm],
        out_specs=[vm] * 5,
        scratch_shapes=scratch,
        compiler_params=pltpu.CompilerParams(
            collective_id=0, has_side_effects=True, vmem_limit_bytes=60 * 2**20
        ),
        name="block",
    )(
        latent,
        target,
        conv_weight.reshape(9, 3 * ch, ch),
        gain.reshape(1, ch),
        bias.reshape(1, ch),
    )
    wgrad = jnp.swapaxes(wgrad.reshape(3, 3, 3, ch // nz, ch), 3, 4)
    return decoded, grad_latent, wgrad, ngrad.reshape(ch), bgrad.reshape(ch)


def solution(mesh, nx=4):
    nt, nz = mesh.shape["tm"], mesh.shape["height"]
    ny = nt // (2 * nx)
    in_specs = (P("tm", "height", None, None), P("tm", "height", None, None), P(), P(), P())
    out_specs = (
        P("tm", "height", None, None),
        P("tm", "height", None, None),
        P(None, None, None, None, "height"),
        P(),
        P(),
    )
    return jax.shard_map(
        functools.partial(per_device, nx, ny, nz),
        mesh=mesh,
        in_specs=in_specs,
        out_specs=out_specs,
        check_vma=False,
    )
```

time: 527 us -> 95 us (0.18)
  blocking collectives: 234 us -> 0 us
  waiting for transfers between devices: 199 us -> 0 us
  Pallas kernels: 0 us -> 86 us
  matrix products: 41.8 us -> 0 us
  between operations: 14.7 us -> 0.64 us
  starting transfers between devices: 12.9 us -> 0 us
  local copies, waits for them, and re-layouts: 15.6 us -> 8.06 us
  other arithmetic: 7.53 us -> 0 us
    psum x3 -> x0, blocking collectives: 234 us -> none  [the longest x1 81.4 us: per_device(): lax.psum(jnp.sum(group_view, axis=(0, 2)), ('tm', 'height')) / total]
    psum x1 -> x0, waiting for transfers between devices: 185 us -> none  [per_device(): summed_w = lax.psum(partial_w, ('tm', 'height'))]
    pallas_call x0 -> x1, Pallas kernels: none -> 86 us  [per_device(): pl.pallas_call(functools.partial(kernel, nx, ny, nz, size), out_shape=out...]
    dot_general x81 -> x0, matrix products: 41.8 us -> none  [the longest x27 27.3 us: per_device(): lax.dot_general(piece, grad_half, (((0,), (0,)), ((), ())), preferred_ele...]
    ppermute x6 -> x0, waiting for transfers between devices: 14.4 us -> none  [the longest x2 10.9 us: shifted(): lax.ppermute(value, axis, [(source, source + steps) for source in range(i...]
    ppermute x6 -> x0, starting transfers between devices: 12.9 us -> none  [the longest x2 5.13 us: extended(): before = lax.ppermute(last, axis, up)]
    reshape x1 -> x0, local copies, waits for them, and re-layouts: 8.09 us -> none  [per_device(): partial_w = jnp.stack(taps).reshape(3, 3, 3, channel_count, channel_count)]
    unnamed x12 -> x5, local copies, waits for them, and re-layouts: 2.41 us -> 8.06 us
  transfers between devices with their start and end apart: 7 -> 0, of which waited for: 4 -> 0; matrix products, arithmetic and copies ran while one was open for 4% -> 0% of each run, Pallas kernels for 0% -> 0%
where the time goes in v1:
time: 95 us; the launch traced here: 94.7 us
  Pallas kernels  86 us (91%)
  local copies, waits for them, and re-layouts  8.06 us (8%)
    pallas_call x1, Pallas kernels, per_device(): pl.pallas_call(functools.partial(kernel, nx, ny, nz, size), out_shape=out...  86 us
    unnamed x5, local copies, waits for them, and re-layouts  8.06 us

profile of v1, /device:TPU:1, one launch (start us, length us, event | category | flops | bytes accessed | tf_op | source)
XLA Modules:
  0.0 94.7 jit_solution(11256936457263231476)
XLA Ops:
  0.6 86.0 %block.1 = (bf16[2,4,80,256]{3,2,1,0:T(8,128)(2,1)}, bf16[2,4,80,256]{3,2,1,0:T(8,128)(2,1)}, f32[9,3,32,256]{3,2,1,0:T(8,128)}, f32[1,256]{1,0:T(1,128)}, f32[1,256]{1,0:T(1,128)}) custom-call(bf16[2,4,80,256]{3,2,1,0:T(8,128)(2,1)} %latent.1, bf16[2,4,80,256]{3,2,1,0:T(8,128)(2,1)} %target_hbm.1, bf16[9,768,256]{2,1,0:T(8,128)(2,1)} %bitcast.8, ...), custom_call_target="tpu_custom_call" | custom-call | tf_op jit(solution)/shard_map/block/pallas_call | solution.py:600
  86.7 1.7 %copy.15 = bf16[2,4,80,256]{3,2,1,0:T(8,128)(2,1)} copy(bf16[2,4,80,256]{3,2,1,0:T(8,128)(2,1)} %get-tuple-element.20) | data formatting | bytes 655360
  88.4 1.7 %copy.16 = bf16[2,4,80,256]{3,2,1,0:T(8,128)(2,1)} copy(bf16[2,4,80,256]{3,2,1,0:T(8,128)(2,1)} %get-tuple-element.21) | data formatting | bytes 655360
  90.1 2.2 %copy.17 = f32[3,3,3,256,32]{3,4,2,1,0:T(8,128)} copy(f32[3,3,3,256,32]{3,4,2,1,0:T(8,128)} %bitcast.9) | data formatting | bytes 1769472
  92.3 1.2 %copy.18 = f32[256]{0:T(256)} copy(f32[256]{0:T(256)} %bitcast.11) | data formatting | bytes 2048
  93.5 1.2 %copy.19 = f32[256]{0:T(256)} copy(f32[256]{0:T(256)} %bitcast.10) | data formatting | bytes 2048

commit v2 on v1

v2 whole, which is shorter than its diff:
```python
import functools

import jax
import jax.numpy as jnp
from jax import lax
from jax.experimental import pallas as pl
from jax.experimental.pallas import tpu as pltpu
from jax.sharding import PartitionSpec as P

NORM_GROUPS = 32
EPS = 1e-06
MESH = pl.DeviceIdType.MESH
F32 = jnp.float32
BF16 = jnp.bfloat16
TAPS = 9


def group_sum(v):
    lane = lax.broadcasted_iota(jnp.int32, v.shape, 1)
    width = v.shape[1]
    for k in (1, 2, 4):
        other = jnp.where(
            lax.rem(lax.div(lane, k), 2) == 1,
            pltpu.roll(v, k, 1),
            pltpu.roll(v, width - k, 1),
        )
        v = v + other
    return v


def pack(a, b):
    half = a.shape[1] // 2
    return jnp.concatenate(
        [a[:, :half], a[:, half:], b[:, :half], b[:, half:], jnp.zeros((4, half), F32)], axis=0
    )


def unpack(v):
    a = jnp.concatenate([v[0:1], v[1:2]], axis=1)
    b = jnp.concatenate([v[2:3], v[3:4]], axis=1)
    return a, b


def kernel(
    nx, ny, nz, shape,
    latent_hbm, target_hbm, w_hbm, gain_hbm, bias_hbm,
    decoded_hbm, grad_latent_hbm, wgrad_hbm, ngrad_hbm, bgrad_hbm,
    L, A, G, graw, g32, acc, W, WT, target, gain_ref, bias_ref,
    decoded, grad_latent, wgrad, ngrad, bgrad,
    gta, gtb, DP, DZ, CP, CZ,
    PH, PF, ZH, ZF, Q2, Q, Q3, ZX, XG, AR,
    in_sem, out_sem, lat_s, lat_r, gh_s, gh_r, ar_s, ar_r, co_s, co_r,
    p_s, p_r, z_s, z_r, q_s, q_r, q3_s, q3_r, zx_s, zx_r, xg_s, xg_r, cg_s, cg_r,
):
    t = lax.axis_index("tm")
    z = lax.axis_index("height")
    nt = 2 * nx * ny
    core = lax.rem(t, 2)
    x = lax.rem(lax.div(t, 2), nx)
    y = lax.div(t, 2 * nx)
    frames, rows, width, ch = shape
    other = 1 - core

    def at(yy, xx, cc):
        return (yy * nx + xx) * 2 + cc

    def remote(src, dst, ss, rs, tt, zz):
        return pltpu.make_async_remote_copy(
            src_ref=src, dst_ref=dst, send_sem=ss, recv_sem=rs,
            device_id=(tt, zz), device_id_type=MESH,
        )

    def loop(lo, hi, f):
        def step(i, c):
            f(i)
            return c

        lax.fori_loop(lo, hi, step, 0)

    up_t, dn_t = lax.rem(t + 1, nt), lax.rem(t + nt - 1, nt)
    up_z, dn_z = lax.rem(z + 1, nz), lax.rem(z + nz - 1, nz)

    latent = L.at[pl.ds(frames, frames), pl.ds(1, rows)]
    latent_in = pltpu.make_async_copy(latent_hbm, latent, in_sem.at[0])
    latent_in.start()

    n1, n2 = 2 * nz, nx * ny
    me1, me2 = core * nz + z, y * nx + x

    def peer1(k):
        p = lax.rem(me1 + k, n1)
        return at(y, x, lax.div(p, nz)), lax.rem(p, nz)

    def peer2(k):
        p = lax.rem(me2 + k, n2)
        return p * 2 + core, z

    barrier = pltpu.get_barrier_semaphore()

    def greet(tt, zz):
        pl.semaphore_signal(barrier, inc=1, device_id=(tt, zz), device_id_type=MESH)

    loop(1, n1, lambda k: greet(*peer1(k)))
    loop(1, n2, lambda k: greet(*peer2(k)))
    for tt in (up_t, dn_t):
        for zz in (dn_z, z, up_z):
            greet(tt, zz)

    gain_in = pltpu.make_async_copy(gain_hbm, gain_ref, in_sem.at[1])
    bias_in = pltpu.make_async_copy(bias_hbm, bias_ref, in_sem.at[2])
    weights_in = pltpu.make_async_copy(w_hbm, W, in_sem.at[3])
    target_in = pltpu.make_async_copy(target_hbm, target, in_sem.at[4])
    for c in (gain_in, bias_in, weights_in, target_in):
        c.start()
    latent_in.wait()

    def eights(v):
        return jnp.sum(v.reshape(width // 8, 8, ch), axis=0)

    def sum_rows(i, total):
        return total + eights(latent[lax.div(i, rows), lax.rem(i, rows)].astype(F32))

    count = frames * rows * width * 8
    total = lax.fori_loop(0, frames * rows, sum_rows, jnp.zeros((8, ch), F32))
    mean_l = group_sum(jnp.sum(total, axis=0, keepdims=True)) / count

    def sum_squares(i, total):
        v = latent[lax.div(i, rows), lax.rem(i, rows)].astype(F32) - mean_l
        return total + eights(v * v)

    total = lax.fori_loop(0, frames * rows, sum_squares, jnp.zeros((8, ch), F32))
    sq_l = group_sum(jnp.sum(total, axis=0, keepdims=True))

    pl.semaphore_wait(barrier, (n1 - 1) + (n2 - 1) + 6)

    def exchange(stage, k):
        me, peer = (me1, peer1) if stage % 2 == 0 else (me2, peer2)
        slot = AR.at[stage, me]
        return remote(slot, slot, ar_s.at[stage, k], ar_r.at[stage, k], *peer(k))

    def spread_out(stage, value):
        me, n = (me1, n1) if stage % 2 == 0 else (me2, n2)
        AR[stage, me] = value
        loop(1, n, lambda k: exchange(stage, k).start())

    def gather_in(stage):
        n = n1 if stage % 2 == 0 else n2
        loop(1, n, lambda k: exchange(stage, k).wait())
        return n

    def plain_total(stage, n):
        total = AR[stage, 0]
        for k in range(1, n):
            total = total + AR[stage, k]
        return total

    def moments(stage, n, members):
        mean = plain_total(stage, n)[0:2] / n
        sq = jnp.zeros_like(mean)
        for k in range(n):
            d = AR[stage, k, 0:2] - mean
            sq = sq + (AR[stage, k, 2:4] + (d * d) * members)
        return jnp.concatenate([mean, sq, jnp.zeros((4, mean.shape[1]), F32)], axis=0)

    spread_out(0, pack(mean_l, sq_l))

    def halo(block, buf, first, away, tt, ss, rs):
        edge0, edge1 = block.at[:, 0], block.at[:, rows - 1]
        mine, theirs = pl.ds(first, frames), pl.ds(away, frames)
        return [
            remote(block, buf.at[theirs, pl.ds(1, rows)], ss.at[0], rs.at[0], tt, z),
            remote(edge1, buf.at[mine, 0], ss.at[1], rs.at[1], t, up_z),
            remote(edge0, buf.at[mine, rows + 1], ss.at[2], rs.at[2], t, dn_z),
            remote(edge1, buf.at[theirs, 0], ss.at[3], rs.at[3], tt, up_z),
            remote(edge0, buf.at[theirs, rows + 1], ss.at[4], rs.at[4], tt, dn_z),
        ]

    lat_halo = halo(latent, L, frames, 0, up_t, lat_s, lat_r)
    for c in lat_halo:
        c.start()

    def flip(u):
        for kc in range(3):
            WT[8 - u, (2 - kc) * ch : (3 - kc) * ch, :] = W[u, kc * ch : (kc + 1) * ch, :].T

    n = gather_in(0)
    spread_out(1, moments(0, n, count))
    weights_in.wait()
    loop(0, TAPS, flip)
    gain_in.wait()
    bias_in.wait()
    n = gather_in(1)
    mean, sq = unpack(moments(1, n, count * n1))
    everything = count * n1 * n2
    rstd = lax.rsqrt(sq / everything + EPS)
    gain, bias = gain_ref[...], bias_ref[...]
    scale = rstd * gain

    for c in lat_halo:
        c.wait()

    col = lax.broadcasted_iota(jnp.int32, (width, ch), 0)

    def store_shifts(buf, f, r, v):
        buf[f, r, :, 0:ch] = jnp.where(col == 0, 0.0, pltpu.roll(v, 1, 0)).astype(BF16)
        buf[f, r, :, ch : 2 * ch] = v.astype(BF16)
        buf[f, r, :, 2 * ch : 3 * ch] = jnp.where(
            col == width - 1, 0.0, pltpu.roll(v, width - 1, 0)
        ).astype(BF16)

    def inside(f, r, lone, edge):
        top = jnp.logical_or(r > 0, z > 0)
        low = jnp.logical_or(r < rows + 1, z < nz - 1)
        return jnp.logical_and(jnp.logical_or(lone, edge), jnp.logical_and(top, low))

    def activate(i):
        f, r = lax.div(i, rows + 2), lax.rem(i, rows + 2)
        zz = (L[f, r].astype(F32) - mean) * scale + bias
        v = zz / (1.0 + jnp.exp(-zz))
        keep = inside(f, r, f >= frames, t > 0)
        store_shifts(A, f, r, jnp.where(keep, v, 0.0))

    loop(0, 2 * frames * (rows + 2), activate)

    size = frames * rows * width

    def piece(buf, u):
        kt, kr = lax.div(u, 3), lax.rem(u, 3)
        return buf[pl.ds(kt, frames), pl.ds(kr, rows)].reshape(size, 3 * ch)

    def conv(buf, w):
        acc[...] = jnp.dot(piece(buf, 0), w[0], preferred_element_type=F32)

        def tap(u):
            acc[...] += jnp.dot(piece(buf, u), w[u], preferred_element_type=F32)

        loop(1, TAPS, tap)

    conv(A, W)
    target_in.wait()

    def finish(i):
        f, r = lax.div(i, rows), lax.rem(i, rows)
        at_row = pl.ds(pl.multiple_of(i * width, 16), width)
        out = latent[f, r].astype(F32) + acc[at_row, :]
        decoded[f, r] = out.astype(BF16)
        g = out - target[f, r].astype(F32)
        g32[at_row, :] = g
        graw[f, 1 + r] = g.astype(BF16)

    loop(0, frames * rows, finish)

    own = graw.at[pl.ds(0, frames), pl.ds(1, rows)]
    g_halo = halo(own, graw, 0, frames, dn_t, gh_s, gh_r)
    for c in g_halo:
        c.start()
    decoded_out = pltpu.make_async_copy(decoded, decoded_hbm, out_sem.at[0])
    decoded_out.start()

    per = ch // (nx * nz)
    half = ch // 2
    for b in range(ch // 128):
        for q in range(size // 128):
            cols = slice(q * 128, (q + 1) * 128)
            block = g32[cols, b * 128 : (b + 1) * 128].T
            gtb[b * 128 : (b + 1) * 128, cols] = block
            for i in range(128 // per):
                zz, cc = divmod(b * (128 // per) + i, nx)
                gta[(cc * nz + zz) * per : (cc * nz + zz + 1) * per, cols] = (
                    block[i * per : (i + 1) * per]
                )

    def core_p(u):
        return remote(DP.at[other, u], CP.at[u], co_s.at[u], co_r.at[u], at(y, x, other), z)

    def core_z():
        return remote(DZ.at[other], CZ, co_s.at[8], co_r.at[8], at(y, x, other), z)

    def kernel_term(gt, unit, store):
        res = jnp.dot(gt[...].astype(BF16), piece(A, unit), preferred_element_type=F32)
        for kc in range(3):
            for h in range(2):
                lo = kc * ch + h * half
                store(h, kc, res[:, lo : lo + half])

    def term_p(u):
        def store(h, kc, v):
            DP[h, u, :, :, kc] = v.reshape(nx, nz, per, half)

        kernel_term(gta, u, store)
        core_p(u).start()

    def term_z():
        def store(h, kc, v):
            DZ[h, :, :, kc] = v.reshape(nz, nx, per, half)

        kernel_term(gtb, 8, store)
        core_z().start()

    def along(u, d):
        s = lax.div(u, 4)
        xx = lax.rem(x + (1 - s) * d + nx, nx)
        yy = lax.rem(y + s * d + ny, ny)
        return x * (1 - s) + y * s, at(yy, xx, core)

    def ring_p(u, step):
        me, up = along(u, 1)
        _, down = along(u, -1)
        sems = [(p_s.at[u, step, d], p_r.at[u, step, d]) for d in range(2)]
        if step == 0:
            far = DP.at[core, u, lax.rem(me + 2, 4)]
            return [
                remote(far.at[pl.ds(0, nz // 2)], PH.at[u, 0], *sems[0], up, z),
                remote(far.at[pl.ds(nz // 2, nz // 2)], PH.at[u, 1], *sems[1], down, z),
            ]
        return [
            remote(DP.at[core, u, lax.rem(me + 1, 4)], PF.at[u, 0], *sems[0], up, z),
            remote(DP.at[core, u, lax.rem(me + 3, 4)], PF.at[u, 1], *sems[1], down, z),
        ]

    def recv_p(u, step):
        me, _ = along(u, 1)
        for c in ring_p(u, step):
            c.wait_recv()
        if step == 0:
            right, left = lax.rem(me + 1, 4), lax.rem(me + 3, 4)
            h = nz // 2
            DP[core, u, right, 0:h] = DP[core, u, right, 0:h] + PH[u, 0]
            DP[core, u, left, h:nz] = DP[core, u, left, h:nz] + PH[u, 1]
        else:
            DP[core, u, me] = DP[core, u, me] + PF[u, 0] + PF[u, 1]

    def order(i):
        return lax.rem(i, 2) * 4 + lax.div(i, 2)

    def first_p(u):
        core_p(u).wait_recv()
        DP[core, u] = DP[core, u] + CP[u]
        for c in ring_p(u, 0):
            c.start()

    sz = nz // 2

    def ring_z(step):
        sems = [(z_s.at[step, d], z_r.at[step, d]) for d in range(2)]
        if step == 0:
            far = DZ.at[core, lax.rem(z + sz, nz)]
            return [
                remote(far.at[pl.ds(0, nx // 2)], ZH.at[0], *sems[0], t, up_z),
                remote(far.at[pl.ds(nx // 2, nx // 2)], ZH.at[1], *sems[1], t, dn_z),
            ]
        up, down = lax.rem(z + sz - step, nz), lax.rem(z + nz - sz + step, nz)
        return [
            remote(DZ.at[core, up], ZF.at[step - 1, 0], *sems[0], t, up_z),
            remote(DZ.at[core, down], ZF.at[step - 1, 1], *sems[1], t, dn_z),
        ]

    def recv_z(step):
        for c in ring_z(step):
            c.wait_recv()
        left = lax.rem(z + nz - 1 + sz - step, nz)
        right = lax.rem(z + nz + 1 - sz + step, nz)
        if step == 0:
            h = nx // 2
            DZ[core, left, 0:h] = DZ[core, left, 0:h] + ZH[0]
            DZ[core, right, h:nx] = DZ[core, right, h:nx] + ZH[1]
        else:
            DZ[core, left] = DZ[core, left] + ZF[step - 1, 0]
            DZ[core, right] = DZ[core, right] + ZF[step - 1, 1]
        if step + 1 < sz:
            for c in ring_z(step + 1):
                c.start()

    term_p(order(0))

    def term_and_first(i):
        term_p(order(i))
        first_p(order(i - 1))

    loop(1, 8, term_and_first)
    term_z()
    first_p(7)
    core_z().wait_recv()
    DZ[core] = DZ[core] + CZ[...]
    for c in ring_z(0):
        c.start()

    def wave_0(i):
        u = order(i)
        recv_p(u, 0)
        for c in ring_p(u, 1):
            c.start()

    def cross(s, k):
        yy = lax.rem(y + (1 - s) * k, ny)
        xx = lax.rem(x + s * k, nx)
        me = x * (1 - s) + y * s
        u = 4 * s + yy * (1 - s) + xx * s
        return remote(
            DP.at[core, u, me], Q2.at[s, k], q_s.at[s, k], q_r.at[s, k], at(yy, xx, core), z
        )

    def wave_1(i):
        u = order(i)
        recv_p(u, 1)
        s, v = lax.div(u, 4), lax.rem(u, 4)
        here = y * (1 - s) + x * s

        @pl.when(v != here)
        def _():
            cross(s, lax.rem(v - here + 4, 4)).start()

    def sum_z(k):
        c = lax.rem(z + k, nz)
        return remote(Q.at[c], Q3.at[k], q3_s.at[k], q3_r.at[k], t, c)

    def wave_2():
        for s in range(2):
            loop(1, 4, lambda k: cross(s, k).wait_recv())
            me, here = (x, y) if s == 0 else (y, x)
            Q[:, s] = DP[core, 4 * s + here, me] + Q2[s, 1] + Q2[s, 2] + Q2[s, 3]
        loop(1, nz, lambda k: sum_z(k).start())

    def z_to_x(k):
        xx = lax.rem(x + k, nx)
        return remote(
            DZ.at[core, z, xx], ZX.at[k], zx_s.at[k], zx_r.at[k], at(y, xx, core), z
        )

    me_xy = y * nx + x

    def publish(k):
        p = lax.rem(me_xy + k, n2)
        slot = XG.at[me_xy, core]
        return remote(slot, slot, xg_s.at[k], xg_r.at[k], p * 2 + core, z)

    def to_core(k):
        slot = XG.at[lax.rem(me_xy + n2 - k, n2), core]
        return remote(slot, slot, cg_s.at[k], cg_r.at[k], at(y, x, other), z)

    def wave_3():
        loop(1, nx, lambda k: z_to_x(k).wait_recv())
        total = DZ[core, z, x]
        for k in range(1, nx):
            total = total + ZX[k]
        XG[me_xy, core, 2] = total
        loop(1, nz, lambda k: sum_z(k).wait_recv())
        total = Q[z]
        for k in range(1, nz):
            total = total + Q3[k]
        XG[me_xy, core, 0:2] = total
        loop(1, n2, lambda k: publish(k).start())
        to_core(0).start()

    loop(0, 8, wave_0)
    recv_z(0)

    for c in g_halo:
        c.wait()

    def shift_gradient(i):
        f, r = lax.div(i, rows + 2), lax.rem(i, rows + 2)
        keep = inside(f, r, f < frames, t < nt - 1)
        store_shifts(G, f, r, jnp.where(keep, graw[f, r].astype(F32), 0.0))

    loop(0, 2 * frames * (rows + 2), shift_gradient)
    for step in range(1, min(2, sz)):
        recv_z(step)
    conv(G, WT)
    for step in range(2, min(3, sz)):
        recv_z(step)

    def through_norm(i, carry):
        s0, s1 = carry
        f, r = lax.div(i, rows), lax.rem(i, rows)
        at_row = pl.ds(pl.multiple_of(i * width, 16), width)
        d = latent[f, r].astype(F32) - mean
        zz = d * scale + bias
        sig = 1.0 / (1.0 + jnp.exp(-zz))
        gz = acc[at_row, :] * sig * (1.0 + zz * (1.0 - sig))
        acc[at_row, :] = gz
        return s0 + eights(gz), s1 + eights(gz * (d * rstd))

    zero = jnp.zeros((8, ch), F32)
    s0, s1 = lax.fori_loop(0, frames * rows, through_norm, (zero, zero))
    spread_out(2, pack(jnp.sum(s0, axis=0, keepdims=True), jnp.sum(s1, axis=0, keepdims=True)))
    for step in range(3, sz):
        recv_z(step)
    loop(1, nx, lambda k: z_to_x(k).start())
    loop(0, 8, wave_1)
    n = gather_in(2)
    spread_out(3, plain_total(2, n))
    wave_2()
    n = gather_in(3)
    s0, s1 = unpack(plain_total(3, n))
    bgrad[...] = s0
    ngrad[...] = s1
    m1 = group_sum(s0 * gain) / everything
    m2 = group_sum(s1 * gain) / everything

    def to_input(i):
        f, r = lax.div(i, rows), lax.rem(i, rows)
        at_row = pl.ds(pl.multiple_of(i * width, 16), width)
        xhat = (latent[f, r].astype(F32) - mean) * rstd
        gx = acc[at_row, :] * gain
        grad_latent[f, r] = (g32[at_row, :] + rstd * (gx - m1 - xhat * m2)).astype(BF16)

    loop(0, frames * rows, to_input)
    outs = [
        decoded_out,
        pltpu.make_async_copy(grad_latent, grad_latent_hbm, out_sem.at[1]),
        pltpu.make_async_copy(ngrad, ngrad_hbm, out_sem.at[2]),
        pltpu.make_async_copy(bgrad, bgrad_hbm, out_sem.at[3]),
        pltpu.make_async_copy(wgrad, wgrad_hbm, out_sem.at[4]),
    ]
    for c in outs[1:4]:
        c.start()

    wave_3()

    def pass_on(k):
        publish(k).wait_recv()
        to_core(k).start()

    loop(1, n2, pass_on)
    loop(0, n2, lambda k: to_core(k).wait_recv())
    for cc in range(2):
        lanes = slice(cc * half, (cc + 1) * half)
        for xx in range(nx):
            for yy in range(ny):
                p = yy * nx + xx
                wgrad[yy, :, xx * per : (xx + 1) * per, lanes] = XG[p, cc, 0]
                wgrad[4 + xx, :, yy * per : (yy + 1) * per, lanes] = XG[p, cc, 1]
            total = XG[xx, cc, 2]
            for yy in range(1, ny):
                total = total + XG[yy * nx + xx, cc, 2]
            wgrad[8, :, xx * per : (xx + 1) * per, lanes] = total
    outs[4].start()

    def drain(u):
        core_p(u).wait_send()
        for step in range(2):
            for c in ring_p(u, step):
                c.wait_send()

    loop(0, 8, drain)
    core_z().wait_send()
    for step in range(sz):
        for c in ring_z(step):
            c.wait_send()

    def drain_cross(k):
        cross(0, k).wait_send()
        cross(1, k).wait_send()
        z_to_x(k).wait_send()

    loop(1, 4, drain_cross)
    loop(1, nz, lambda k: sum_z(k).wait_send())
    loop(1, n2, lambda k: publish(k).wait_send())
    loop(0, n2, lambda k: to_core(k).wait_send())
    for c in outs:
        c.wait()


def hand_over(*refs):
    n = len(refs) // 3
    given, out, held, sem = refs[:n], refs[n : 2 * n], refs[2 * n : 3 * n], refs[-1]
    into = [pltpu.make_async_copy(given[i], held[i], sem.at[0, i]) for i in range(n)]
    onto = [pltpu.make_async_copy(held[i], out[i], sem.at[1, i]) for i in range(n)]
    for c in into:
        c.start()
    for a, b in zip(into, onto):
        a.wait()
        b.start()
    for c in onto:
        c.wait()


def per_device(nx, ny, nz, latent, target, conv_weight, gain, bias):
    frames, rows, width, ch = latent.shape
    size = frames * rows * width
    per, half = ch // (nx * nz), ch // 2
    sz, n2 = nz // 2, nx * ny
    tile = (3, per, half)
    V, D = pltpu.VMEM, pltpu.SemaphoreType.DMA
    padded = (2 * frames, rows + 2, width)
    block = (frames, rows, width, ch)
    most = max(2 * nz, n2)
    scratch = [
        V(padded + (ch,), BF16),
        V(padded + (3 * ch,), BF16),
        V(padded + (3 * ch,), BF16),
        V(padded + (ch,), BF16),
        V((size, ch), F32),
        V((size, ch), F32),
        V((TAPS, 3 * ch, ch), BF16),
        V((TAPS, 3 * ch, ch), BF16),
        V(block, BF16),
        V((1, ch), F32),
        V((1, ch), F32),
        V(block, BF16),
        V(block, BF16),
        V((TAPS, 3, ch // nz, ch), F32),
        V((1, ch), F32),
        V((1, ch), F32),
        V((ch, size), F32),
        V((ch, size), F32),
        V((2, 8, nx, nz) + tile, F32),
        V((2, nz, nx) + tile, F32),
        V((8, nx, nz) + tile, F32),
        V((nz, nx) + tile, F32),
        V((8, 2, nz // 2) + tile, F32),
        V((8, 2, nz) + tile, F32),
        V((2, nx // 2) + tile, F32),
        V((max(sz - 1, 1), 2, nx) + tile, F32),
        V((2, 4, nz) + tile, F32),
        V((nz, 2) + tile, F32),
        V((nz, 2) + tile, F32),
        V((nx,) + tile, F32),
        V((n2, 2, 3) + tile, F32),
        V((4, most, 8, half), F32),
        D((5,)), D((5,)),
        D((5,)), D((5,)), D((5,)), D((5,)),
        D((4, most)), D((4, most)),
        D((9,)), D((9,)),
        D((8, 2, 2)), D((8, 2, 2)),
        D((sz, 2)), D((sz, 2)),
        D((2, 4)), D((2, 4)),
        D((nz,)), D((nz,)),
        D((nx,)), D((nx,)),
        D((n2,)), D((n2,)), D((n2,)), D((n2,)),
    ]
    anywhere = pl.BlockSpec(memory_space=pl.ANY)
    shapes = [
        jax.ShapeDtypeStruct(latent.shape, BF16),
        jax.ShapeDtypeStruct(latent.shape, BF16),
        jax.ShapeDtypeStruct((TAPS, 3, ch // nz, ch), F32),
        jax.ShapeDtypeStruct((1, ch), F32),
        jax.ShapeDtypeStruct((1, ch), F32),
    ]
    results = pl.pallas_call(
        functools.partial(kernel, nx, ny, nz, latent.shape),
        out_shape=shapes,
        in_specs=[anywhere] * 5,
        out_specs=[anywhere] * 5,
        scratch_shapes=scratch,
        compiler_params=pltpu.CompilerParams(
            collective_id=0, has_side_effects=True, vmem_limit_bytes=60 * 2**20
        ),
        name="block",
    )(
        latent,
        target,
        conv_weight.reshape(TAPS, 3 * ch, ch),
        gain.reshape(1, ch),
        bias.reshape(1, ch),
    )
    decoded, grad_latent, wgrad, ngrad, bgrad = pl.pallas_call(
        hand_over,
        out_shape=shapes,
        in_specs=[anywhere] * 5,
        out_specs=[anywhere] * 5,
        scratch_shapes=[V(o.shape, o.dtype) for o in shapes] + [D((2, 5))],
        name="hand_over",
    )(*results)
    wgrad = jnp.swapaxes(wgrad.reshape(3, 3, 3, ch // nz, ch), 3, 4)
    return decoded, grad_latent, wgrad, ngrad.reshape(ch), bgrad.reshape(ch)


def solution(mesh, nx=4):
    nt, nz = mesh.shape["tm"], mesh.shape["height"]
    ny = nt // (2 * nx)
    in_specs = (P("tm", "height", None, None), P("tm", "height", None, None), P(), P(), P())
    out_specs = (
        P("tm", "height", None, None),
        P("tm", "height", None, None),
        P(None, None, None, None, "height"),
        P(),
        P(),
    )
    return jax.shard_map(
        functools.partial(per_device, nx, ny, nz),
        mesh=mesh,
        in_specs=in_specs,
        out_specs=out_specs,
        check_vma=False,
    )
```

time: 95 us -> 80.6 us (0.85)
  local copies, waits for them, and re-layouts: 8.06 us -> 0 us
  Pallas kernels: 86 us -> 79.8 us
    unnamed x5 -> x0, local copies, waits for them, and re-layouts: 8.06 us -> none
    pallas_call x1 -> x2, Pallas kernels: 86 us -> 79.8 us  [the longest x1 77.5 us: per_device(): pl.pallas_call(functools.partial(kernel, nx, ny, nz, latent.shape), out_s...]
where the time goes in v2:
time: 80.6 us; the launch traced here: 80.5 us
  Pallas kernels  79.8 us (99%)
    pallas_call x1, Pallas kernels, per_device(): pl.pallas_call(functools.partial(kernel, nx, ny, nz, latent.shape), out_s...  77.5 us
    pallas_call x1, Pallas kernels, per_device(): pl.pallas_call(hand_over, out_shape=shapes, in_specs=[anywhere] * 5, out_...  2.38 us

profile of v2, /device:TPU:1, one launch (start us, length us, event | category | flops | bytes accessed | tf_op | source)
XLA Modules:
  0.0 80.5 jit_solution(8740912649399891170)
XLA Ops:
  0.6 77.5 %block.1 = (bf16[2,4,80,256]{3,2,1,0:T(8,128)(2,1)}, bf16[2,4,80,256]{3,2,1,0:T(8,128)(2,1)}, f32[9,3,32,256]{3,2,1,0:T(8,128)}, f32[1,256]{1,0:T(1,128)}, f32[1,256]{1,0:T(1,128)}) custom-call(bf16[2,4,80,256]{3,2,1,0:T(8,128)(2,1)} %latent_hbm.1, bf16[2,4,80,256]{3,2,1,0:T(8,128)(2,1)} %target_hbm.1, bf16[9,768,256]{2,1,0:T(8,128)(2,1)} %bitcast.8, ...), custom_call_target="tpu_custom_call" | custom-call | tf_op jit(solution)/shard_map/block/pallas_call | solution.py:641
  78.1 2.4 %hand_over.1 = (bf16[2,4,80,256]{3,2,1,0:T(8,128)(2,1)}, bf16[2,4,80,256]{3,2,1,0:T(8,128)(2,1)}, f32[9,3,32,256]{3,2,1,0:T(8,128)}, f32[1,256]{1,0:T(1,128)}, f32[1,256]{1,0:T(1,128)}) custom-call(bf16[2,4,80,256]{3,2,1,0:T(8,128)(2,1)} %get-tuple-element.15.refs_0_, bf16[2,4,80,256]{3,2,1,0:T(8,128)(2,1)} %get-tuple-element.16.refs_1_, ...), custom_call_target="tpu_custom_call" | custom-call | tf_op jit(solution)/shard_map/hand_over/pallas_call | solution.py:658

commit v3 on v2

--- a/solution.py
+++ b/solution.py
@@ -20,7 +20,7 @@
     width = v.shape[1]
     for k in (1, 2, 4):
         other = jnp.where(
-            lax.rem(lax.div(lane, k), 2) == 1,
+            (lane & k) != 0,
             pltpu.roll(v, k, 1),
             pltpu.roll(v, width - k, 1),
         )
@@ -39,6 +39,12 @@
     a = jnp.concatenate([v[0:1], v[1:2]], axis=1)
     b = jnp.concatenate([v[2:3], v[3:4]], axis=1)
     return a, b
+
+
+FAR_FIRST = (
+    (4, 12, 3, 5, 11, 13, 2, 6, 10, 14, 1, 7, 9, 15, 8),
+    (10, 6, 14, 9, 11, 2, 8, 5, 7, 13, 15, 3, 1, 4, 12),
+)
 
 
 def kernel(
@@ -47,10 +53,11 @@
     decoded_hbm, grad_latent_hbm, wgrad_hbm, ngrad_hbm, bgrad_hbm,
     L, A, G, graw, g32, acc, W, WT, target, gain_ref, bias_ref,
     decoded, grad_latent, wgrad, ngrad, bgrad,
-    gta, gtb, DP, DZ, CP, CZ,
-    PH, PF, ZH, ZF, Q2, Q, Q3, ZX, XG, AR,
+    gta, gtb, gta16, gtb16, DP, DZ, CP, CZ,
+    PH, PF, ZH, ZF, Q2, Q, Q3, ZX, XG, XZ, AR,
     in_sem, out_sem, lat_s, lat_r, gh_s, gh_r, ar_s, ar_r, co_s, co_r,
     p_s, p_r, z_s, z_r, q_s, q_r, q3_s, q3_r, zx_s, zx_r, xg_s, xg_r, cg_s, cg_r,
+    xz_s, xz_r, cz_s, cz_r,
 ):
     t = lax.axis_index("tm")
     z = lax.axis_index("height")
@@ -141,7 +148,9 @@
     def spread_out(stage, value):
         me, n = (me1, n1) if stage % 2 == 0 else (me2, n2)
         AR[stage, me] = value
-        loop(1, n, lambda k: exchange(stage, k).start())
+        for k in FAR_FIRST[stage % 2]:
+            if k < n:
+                exchange(stage, k).start()
 
     def gather_in(stage):
         n = n1 if stage % 2 == 0 else n2
@@ -229,12 +238,17 @@
         return buf[pl.ds(kt, frames), pl.ds(kr, rows)].reshape(size, 3 * ch)
 
     def conv(buf, w):
-        acc[...] = jnp.dot(piece(buf, 0), w[0], preferred_element_type=F32)
-
-        def tap(u):
-            acc[...] += jnp.dot(piece(buf, u), w[u], preferred_element_type=F32)
-
-        loop(1, TAPS, tap)
+        def frame_tap(kt):
+            left = jnp.concatenate([piece(buf, 3 * kt + kr) for kr in range(3)], axis=1)
+            right = w[pl.ds(3 * kt, 3)].reshape(9 * ch, ch)
+            return jnp.dot(left, right, preferred_element_type=F32)
+
+        acc[...] = frame_tap(0)
+
+        def more(kt):
+            acc[...] += frame_tap(kt)
+
+        loop(1, 3, more)
 
     conv(A, W)
     target_in.wait()
@@ -276,8 +290,11 @@
     def core_z():
         return remote(DZ.at[other], CZ, co_s.at[8], co_r.at[8], at(y, x, other), z)
 
+    gta16[...] = gta[...].astype(BF16)
+    gtb16[...] = gtb[...].astype(BF16)
+
     def kernel_term(gt, unit, store):
-        res = jnp.dot(gt[...].astype(BF16), piece(A, unit), preferred_element_type=F32)
+        res = jnp.dot(gt[...], piece(A, unit), preferred_element_type=F32)
         for kc in range(3):
             for h in range(2):
                 lo = kc * ch + h * half
@@ -287,14 +304,14 @@
         def store(h, kc, v):
             DP[h, u, :, :, kc] = v.reshape(nx, nz, per, half)
 
-        kernel_term(gta, u, store)
+        kernel_term(gta16, u, store)
         core_p(u).start()
 
     def term_z():
         def store(h, kc, v):
             DZ[h, :, :, kc] = v.reshape(nz, nx, per, half)
 
-        kernel_term(gtb, 8, store)
+        kernel_term(gtb16, 8, store)
         core_z().start()
 
     def along(u, d):
@@ -371,25 +388,36 @@
             for c in ring_z(step + 1):
                 c.start()
 
-    term_p(order(0))
-
-    def term_and_first(i):
-        term_p(order(i))
-        first_p(order(i - 1))
-
-    loop(1, 8, term_and_first)
-    term_z()
-    first_p(7)
-    core_z().wait_recv()
-    DZ[core] = DZ[core] + CZ[...]
-    for c in ring_z(0):
-        c.start()
-
     def wave_0(i):
         u = order(i)
         recv_p(u, 0)
         for c in ring_p(u, 1):
             c.start()
+
+    term_z()
+    term_p(order(0))
+    term_p(order(1))
+    core_z().wait_recv()
+    DZ[core] = DZ[core] + CZ[...]
+    for c in ring_z(0):
+        c.start()
+
+    def term_2(i):
+        term_p(order(i))
+        first_p(order(i - 2))
+
+    def term_3(i):
+        term_2(i)
+        wave_0(i - 5)
+
+    loop(2, 5, term_2)
+    recv_z(0)
+    loop(5, 8, term_3)
+    first_p(order(6))
+    first_p(order(7))
+    loop(3, 6, wave_0)
+    recv_z(1)
+    loop(6, 8, wave_0)
 
     def cross(s, k):
         yy = lax.rem(y + (1 - s) * k, ny)
@@ -419,7 +447,8 @@
             loop(1, 4, lambda k: cross(s, k).wait_recv())
             me, here = (x, y) if s == 0 else (y, x)
             Q[:, s] = DP[core, 4 * s + here, me] + Q2[s, 1] + Q2[s, 2] + Q2[s, 3]
-        loop(1, nz, lambda k: sum_z(k).start())
+        for k in (4, 3, 5, 2, 6, 1, 7):
+            sum_z(k).start()
 
     def z_to_x(k):
         xx = lax.rem(x + k, nx)
@@ -438,22 +467,35 @@
         slot = XG.at[lax.rem(me_xy + n2 - k, n2), core]
         return remote(slot, slot, cg_s.at[k], cg_r.at[k], at(y, x, other), z)
 
-    def wave_3():
+    def publish_z(k):
+        p = lax.rem(me_xy + k, n2)
+        slot = XZ.at[me_xy, core]
+        return remote(slot, slot, xz_s.at[k], xz_r.at[k], p * 2 + core, z)
+
+    def to_core_z():
+        slot = XZ.at[:, core]
+        return remote(slot, slot, cz_s.at[0], cz_r.at[0], at(y, x, other), z)
+
+    def finish_z():
         loop(1, nx, lambda k: z_to_x(k).wait_recv())
         total = DZ[core, z, x]
         for k in range(1, nx):
             total = total + ZX[k]
-        XG[me_xy, core, 2] = total
+        XZ[me_xy, core] = total
+        for k in FAR_FIRST[1]:
+            publish_z(k).start()
+
+    def wave_3():
         loop(1, nz, lambda k: sum_z(k).wait_recv())
         total = Q[z]
         for k in range(1, nz):
             total = total + Q3[k]
-        XG[me_xy, core, 0:2] = total
-        loop(1, n2, lambda k: publish(k).start())
+        XG[me_xy, core] = total
+        for k in FAR_FIRST[1]:
+            publish(k).start()
         to_core(0).start()
-
-    loop(0, 8, wave_0)
-    recv_z(0)
+        loop(1, n2, lambda k: publish_z(k).wait_recv())
+        to_core_z().start()
 
     for c in g_halo:
         c.wait()
@@ -464,11 +506,10 @@
         store_shifts(G, f, r, jnp.where(keep, graw[f, r].astype(F32), 0.0))
 
     loop(0, 2 * frames * (rows + 2), shift_gradient)
-    for step in range(1, min(2, sz)):
-        recv_z(step)
+    recv_z(2)
     conv(G, WT)
-    for step in range(2, min(3, sz)):
-        recv_z(step)
+    recv_z(3)
+    loop(1, nx, lambda k: z_to_x(k).start())
 
     def through_norm(i, carry):
         s0, s1 = carry
@@ -484,10 +525,8 @@
     zero = jnp.zeros((8, ch), F32)
     s0, s1 = lax.fori_loop(0, frames * rows, through_norm, (zero, zero))
     spread_out(2, pack(jnp.sum(s0, axis=0, keepdims=True), jnp.sum(s1, axis=0, keepdims=True)))
-    for step in range(3, sz):
-        recv_z(step)
-    loop(1, nx, lambda k: z_to_x(k).start())
     loop(0, 8, wave_1)
+    finish_z()
     n = gather_in(2)
     spread_out(3, plain_total(2, n))
     wave_2()
@@ -522,7 +561,9 @@
         publish(k).wait_recv()
         to_core(k).start()
 
-    loop(1, n2, pass_on)
+    for k in (12, 4, 1, 3, 15, 13, 7, 5, 8, 2, 11, 9, 14, 6, 10):
+        pass_on(k)
+    to_core_z().wait_recv()
     loop(0, n2, lambda k: to_core(k).wait_recv())
     for cc in range(2):
         lanes = slice(cc * half, (cc + 1) * half)
@@ -531,9 +572,9 @@
                 p = yy * nx + xx
                 wgrad[yy, :, xx * per : (xx + 1) * per, lanes] = XG[p, cc, 0]
                 wgrad[4 + xx, :, yy * per : (yy + 1) * per, lanes] = XG[p, cc, 1]
-            total = XG[xx, cc, 2]
+            total = XZ[xx, cc]
             for yy in range(1, ny):
-                total = total + XG[yy * nx + xx, cc, 2]
+                total = total + XZ[yy * nx + xx, cc]
             wgrad[8, :, xx * per : (xx + 1) * per, lanes] = total
     outs[4].start()
 
@@ -557,6 +598,8 @@
     loop(1, 4, drain_cross)
     loop(1, nz, lambda k: sum_z(k).wait_send())
     loop(1, n2, lambda k: publish(k).wait_send())
+    loop(1, n2, lambda k: publish_z(k).wait_send())
+    to_core_z().wait_send()
     loop(0, n2, lambda k: to_core(k).wait_send())
     for c in outs:
         c.wait()
@@ -605,6 +648,8 @@
         V((1, ch), F32),
         V((ch, size), F32),
         V((ch, size), F32),
+        V((ch, size), BF16),
+        V((ch, size), BF16),
         V((2, 8, nx, nz) + tile, F32),
         V((2, nz, nx) + tile, F32),
         V((8, nx, nz) + tile, F32),
@@ -617,7 +662,8 @@
         V((nz, 2) + tile, F32),
         V((nz, 2) + tile, F32),
         V((nx,) + tile, F32),
-        V((n2, 2, 3) + tile, F32),
+        V((n2, 2, 2) + tile, F32),
+        V((n2, 2) + tile, F32),
         V((4, most, 8, half), F32),
         D((5,)), D((5,)),
         D((5,)), D((5,)), D((5,)), D((5,)),
@@ -629,6 +675,7 @@
         D((nz,)), D((nz,)),
         D((nx,)), D((nx,)),
         D((n2,)), D((n2,)), D((n2,)), D((n2,)),
+        D((n2,)), D((n2,)), D((1,)), D((1,)),
     ]
     anywhere = pl.BlockSpec(memory_space=pl.ANY)
     shapes = [

time: 80.6 us -> 77.3 us (0.959)
  Pallas kernels: 79.8 us -> 76.5 us
    pallas_call x1, Pallas kernels: 77.5 us -> 74.1 us  [per_device(): pl.pallas_call(functools.partial(kernel, nx, ny, nz, latent.shape), out_s...]
where the time goes in v3:
time: 77.3 us; the launch traced here: 77.2 us
  Pallas kernels  76.5 us (99%)
    pallas_call x1, Pallas kernels, per_device(): pl.pallas_call(functools.partial(kernel, nx, ny, nz, latent.shape), out_s...  74.1 us
    pallas_call x1, Pallas kernels, per_device(): pl.pallas_call(hand_over, out_shape=shapes, in_specs=[anywhere] * 5, out_...  2.38 us

profile of v3, /device:TPU:1, one launch (start us, length us, event | category | flops | bytes accessed | tf_op | source)
XLA Modules:
  0.0 77.2 jit_solution(867048128394721375)
XLA Ops:
  0.6 74.1 %block.1 = (bf16[2,4,80,256]{3,2,1,0:T(8,128)(2,1)}, bf16[2,4,80,256]{3,2,1,0:T(8,128)(2,1)}, f32[9,3,32,256]{3,2,1,0:T(8,128)}, f32[1,256]{1,0:T(1,128)}, f32[1,256]{1,0:T(1,128)}) custom-call(bf16[2,4,80,256]{3,2,1,0:T(8,128)(2,1)} %latent_hbm.1, bf16[2,4,80,256]{3,2,1,0:T(8,128)(2,1)} %target_hbm.1, bf16[9,768,256]{2,1,0:T(8,128)(2,1)} %bitcast.8, ...), custom_call_target="tpu_custom_call" | custom-call | tf_op jit(solution)/shard_map/block/pallas_call | solution.py:688
  74.8 2.4 %hand_over.1 = (bf16[2,4,80,256]{3,2,1,0:T(8,128)(2,1)}, bf16[2,4,80,256]{3,2,1,0:T(8,128)(2,1)}, f32[9,3,32,256]{3,2,1,0:T(8,128)}, f32[1,256]{1,0:T(1,128)}, f32[1,256]{1,0:T(1,128)}) custom-call(bf16[2,4,80,256]{3,2,1,0:T(8,128)(2,1)} %get-tuple-element.15.refs_0_, bf16[2,4,80,256]{3,2,1,0:T(8,128)(2,1)} %get-tuple-element.16.refs_1_, ...), custom_call_target="tpu_custom_call" | custom-call | tf_op jit(solution)/shard_map/hand_over/pallas_call | solution.py:705

commit v4 on v3

--- a/solution.py
+++ b/solution.py
@@ -50,12 +50,11 @@
 def kernel(
     nx, ny, nz, shape,
     latent_hbm, target_hbm, w_hbm, gain_hbm, bias_hbm,
-    decoded_hbm, grad_latent_hbm, wgrad_hbm, ngrad_hbm, bgrad_hbm,
+    decoded, grad_latent, wgrad, ngrad, bgrad,
     L, A, G, graw, g32, acc, W, WT, target, gain_ref, bias_ref,
-    decoded, grad_latent, wgrad, ngrad, bgrad,
     gta, gtb, gta16, gtb16, DP, DZ, CP, CZ,
-    PH, PF, ZH, ZF, Q2, Q, Q3, ZX, XG, XZ, AR,
-    in_sem, out_sem, lat_s, lat_r, gh_s, gh_r, ar_s, ar_r, co_s, co_r,
+    PX, PY, PF, ZH, ZF, Q2, Q, Q3, ZX, XG, XZ, AR,
+    in_sem, lat_s, lat_r, gh_s, gh_r, ar_s, ar_r, co_s, co_r,
     p_s, p_r, z_s, z_r, q_s, q_r, q3_s, q3_r, zx_s, zx_r, xg_s, xg_r, cg_s, cg_r,
     xz_s, xz_r, cz_s, cz_r,
 ):
@@ -268,8 +267,6 @@
     g_halo = halo(own, graw, 0, frames, dn_t, gh_s, gh_r)
     for c in g_halo:
         c.start()
-    decoded_out = pltpu.make_async_copy(decoded, decoded_hbm, out_sem.at[0])
-    decoded_out.start()
 
     per = ch // (nx * nz)
     half = ch // 2
@@ -314,46 +311,46 @@
         kernel_term(gtb16, 8, store)
         core_z().start()
 
-    def along(u, d):
-        s = lax.div(u, 4)
+    cuts = (nz * 6 // 8, nz // 2)
+
+    def along(s, d):
         xx = lax.rem(x + (1 - s) * d + nx, nx)
         yy = lax.rem(y + s * d + ny, ny)
-        return x * (1 - s) + y * s, at(yy, xx, core)
-
-    def ring_p(u, step):
-        me, up = along(u, 1)
-        _, down = along(u, -1)
+        return at(yy, xx, core)
+
+    def ring_p(s, j, step):
+        u = 4 * s + j
+        me, up, down = (x, y)[s], along(s, 1), along(s, -1)
         sems = [(p_s.at[u, step, d], p_r.at[u, step, d]) for d in range(2)]
         if step == 0:
-            far = DP.at[core, u, lax.rem(me + 2, 4)]
+            far, cut, buf = DP.at[core, u, lax.rem(me + 2, 4)], cuts[s], (PX, PY)[s].at[j]
+            head, rest = pl.ds(0, cut), pl.ds(cut, nz - cut)
             return [
-                remote(far.at[pl.ds(0, nz // 2)], PH.at[u, 0], *sems[0], up, z),
-                remote(far.at[pl.ds(nz // 2, nz // 2)], PH.at[u, 1], *sems[1], down, z),
+                remote(far.at[head], buf.at[head], *sems[0], up, z),
+                remote(far.at[rest], buf.at[rest], *sems[1], down, z),
             ]
         return [
             remote(DP.at[core, u, lax.rem(me + 1, 4)], PF.at[u, 0], *sems[0], up, z),
             remote(DP.at[core, u, lax.rem(me + 3, 4)], PF.at[u, 1], *sems[1], down, z),
         ]
 
-    def recv_p(u, step):
-        me, _ = along(u, 1)
-        for c in ring_p(u, step):
+    def recv_p(s, j, step):
+        u, me = 4 * s + j, (x, y)[s]
+        for c in ring_p(s, j, step):
             c.wait_recv()
         if step == 0:
             right, left = lax.rem(me + 1, 4), lax.rem(me + 3, 4)
-            h = nz // 2
-            DP[core, u, right, 0:h] = DP[core, u, right, 0:h] + PH[u, 0]
-            DP[core, u, left, h:nz] = DP[core, u, left, h:nz] + PH[u, 1]
+            cut, buf = cuts[s], (PX, PY)[s]
+            DP[core, u, right, 0:cut] = DP[core, u, right, 0:cut] + buf[j, 0:cut]
+            DP[core, u, left, cut:nz] = DP[core, u, left, cut:nz] + buf[j, cut:nz]
         else:
             DP[core, u, me] = DP[core, u, me] + PF[u, 0] + PF[u, 1]
 
-    def order(i):
-        return lax.rem(i, 2) * 4 + lax.div(i, 2)
-
-    def first_p(u):
+    def first_p(s, j):
+        u = 4 * s + j
         core_p(u).wait_recv()
         DP[core, u] = DP[core, u] + CP[u]
-        for c in ring_p(u, 0):
+        for c in ring_p(s, j, 0):
             c.start()
 
     sz = nz // 2
@@ -388,36 +385,40 @@
             for c in ring_z(step + 1):
                 c.start()
 
-    def wave_0(i):
-        u = order(i)
-        recv_p(u, 0)
-        for c in ring_p(u, 1):
+    def wave_0(j):
+        for s in range(2):
+            recv_p(s, j, 0)
+            for c in ring_p(s, j, 1):
+                c.start()
+
+    def terms(j):
+        for s in range(2):
+            term_p(4 * s + j)
+
+    def terms_and_first(j):
+        for s in range(2):
+            term_p(4 * s + j)
+            first_p(s, j - 2)
+
+    def first_z():
+        core_z().wait_recv()
+        DZ[core] = DZ[core] + CZ[...]
+        for c in ring_z(0):
             c.start()
 
+    def firsts(j):
+        for s in range(2):
+            first_p(s, j)
+
     term_z()
-    term_p(order(0))
-    term_p(order(1))
-    core_z().wait_recv()
-    DZ[core] = DZ[core] + CZ[...]
-    for c in ring_z(0):
-        c.start()
-
-    def term_2(i):
-        term_p(order(i))
-        first_p(order(i - 2))
-
-    def term_3(i):
-        term_2(i)
-        wave_0(i - 5)
-
-    loop(2, 5, term_2)
+    loop(0, 2, terms)
+    first_z()
+    loop(2, 4, terms_and_first)
+    loop(4 - 2, 4, firsts)
+    loop(0, 2, wave_0)
     recv_z(0)
-    loop(5, 8, term_3)
-    first_p(order(6))
-    first_p(order(7))
-    loop(3, 6, wave_0)
+    loop(2, 4, wave_0)
     recv_z(1)
-    loop(6, 8, wave_0)
 
     def cross(s, k):
         yy = lax.rem(y + (1 - s) * k, ny)
@@ -428,15 +429,14 @@
             DP.at[core, u, me], Q2.at[s, k], q_s.at[s, k], q_r.at[s, k], at(yy, xx, core), z
         )
 
-    def wave_1(i):
-        u = order(i)
-        recv_p(u, 1)
-        s, v = lax.div(u, 4), lax.rem(u, 4)
-        here = y * (1 - s) + x * s
-
-        @pl.when(v != here)
-        def _():
-            cross(s, lax.rem(v - here + 4, 4)).start()
+    def wave_1(j):
+        for s in range(2):
+            recv_p(s, j, 1)
+            here = (y, x)[s]
+
+            @pl.when(j != here)
+            def _():
+                cross(s, lax.rem(j - here + 4, 4)).start()
 
     def sum_z(k):
         c = lax.rem(z + k, nz)
@@ -525,7 +525,7 @@
     zero = jnp.zeros((8, ch), F32)
     s0, s1 = lax.fori_loop(0, frames * rows, through_norm, (zero, zero))
     spread_out(2, pack(jnp.sum(s0, axis=0, keepdims=True), jnp.sum(s1, axis=0, keepdims=True)))
-    loop(0, 8, wave_1)
+    loop(0, 4, wave_1)
     finish_z()
     n = gather_in(2)
     spread_out(3, plain_total(2, n))
@@ -545,15 +545,6 @@
         grad_latent[f, r] = (g32[at_row, :] + rstd * (gx - m1 - xhat * m2)).astype(BF16)
 
     loop(0, frames * rows, to_input)
-    outs = [
-        decoded_out,
-        pltpu.make_async_copy(grad_latent, grad_latent_hbm, out_sem.at[1]),
-        pltpu.make_async_copy(ngrad, ngrad_hbm, out_sem.at[2]),
-        pltpu.make_async_copy(bgrad, bgrad_hbm, out_sem.at[3]),
-        pltpu.make_async_copy(wgrad, wgrad_hbm, out_sem.at[4]),
-    ]
-    for c in outs[1:4]:
-        c.start()
 
     wave_3()
 
@@ -576,15 +567,15 @@
             for yy in range(1, ny):
                 total = total + XZ[yy * nx + xx, cc]
             wgrad[8, :, xx * per : (xx + 1) * per, lanes] = total
-    outs[4].start()
-
-    def drain(u):
-        core_p(u).wait_send()
-        for step in range(2):
-            for c in ring_p(u, step):
-                c.wait_send()
-
-    loop(0, 8, drain)
+
+    def drain(j):
+        for s in range(2):
+            core_p(4 * s + j).wait_send()
+            for step in range(2):
+                for c in ring_p(s, j, step):
+                    c.wait_send()
+
+    loop(0, 4, drain)
     core_z().wait_send()
     for step in range(sz):
         for c in ring_z(step):
@@ -601,21 +592,14 @@
     loop(1, n2, lambda k: publish_z(k).wait_send())
     to_core_z().wait_send()
     loop(0, n2, lambda k: to_core(k).wait_send())
-    for c in outs:
-        c.wait()
 
 
 def hand_over(*refs):
-    n = len(refs) // 3
-    given, out, held, sem = refs[:n], refs[n : 2 * n], refs[2 * n : 3 * n], refs[-1]
-    into = [pltpu.make_async_copy(given[i], held[i], sem.at[0, i]) for i in range(n)]
-    onto = [pltpu.make_async_copy(held[i], out[i], sem.at[1, i]) for i in range(n)]
-    for c in into:
+    n = len(refs) // 2
+    copies = [pltpu.make_async_copy(refs[i], refs[n + i], refs[-1].at[i]) for i in range(n)]
+    for c in copies:
         c.start()
-    for a, b in zip(into, onto):
-        a.wait()
-        b.start()
-    for c in onto:
+    for c in copies:
         c.wait()
 
 
@@ -641,11 +625,6 @@
         V(block, BF16),
         V((1, ch), F32),
         V((1, ch), F32),
-        V(block, BF16),
-        V(block, BF16),
-        V((TAPS, 3, ch // nz, ch), F32),
-        V((1, ch), F32),
-        V((1, ch), F32),
         V((ch, size), F32),
         V((ch, size), F32),
         V((ch, size), BF16),
@@ -654,7 +633,8 @@
         V((2, nz, nx) + tile, F32),
         V((8, nx, nz) + tile, F32),
         V((nz, nx) + tile, F32),
-        V((8, 2, nz // 2) + tile, F32),
+        V((4, nz) + tile, F32),
+        V((4, nz) + tile, F32),
         V((8, 2, nz) + tile, F32),
         V((2, nx // 2) + tile, F32),
         V((max(sz - 1, 1), 2, nx) + tile, F32),
@@ -665,7 +645,7 @@
         V((n2, 2, 2) + tile, F32),
         V((n2, 2) + tile, F32),
         V((4, most, 8, half), F32),
-        D((5,)), D((5,)),
+        D((5,)),
         D((5,)), D((5,)), D((5,)), D((5,)),
         D((4, most)), D((4, most)),
         D((9,)), D((9,)),
@@ -687,29 +667,34 @@
     ]
     results = pl.pallas_call(
         functools.partial(kernel, nx, ny, nz, latent.shape),
-        out_shape=shapes,
-        in_specs=[anywhere] * 5,
-        out_specs=[anywhere] * 5,
+        out_shape=[V(o.shape, o.dtype) for o in shapes],
+        in_specs=[pl.BlockSpec(memory_space=pltpu.HBM)] * 5,
+        out_specs=[pl.BlockSpec(memory_space=V)] * 5,
         scratch_shapes=scratch,
         compiler_params=pltpu.CompilerParams(
-            collective_id=0, has_side_effects=True, vmem_limit_bytes=60 * 2**20
+            collective_id=0, has_side_effects=True, vmem_limit_bytes=52 * 2**20
         ),
         name="block",
     )(
-        latent,
-        target,
-        conv_weight.reshape(TAPS, 3 * ch, ch),
-        gain.reshape(1, ch),
-        bias.reshape(1, ch),
+        *(
+            pltpu.with_memory_space_constraint(v, pltpu.HBM)
+            for v in (
+                latent,
+                target,
+                conv_weight.reshape(TAPS, 3 * ch, ch),
+                gain.reshape(1, ch),
+                bias.reshape(1, ch),
+            )
+        )
     )
     decoded, grad_latent, wgrad, ngrad, bgrad = pl.pallas_call(
         hand_over,
         out_shape=shapes,
         in_specs=[anywhere] * 5,
         out_specs=[anywhere] * 5,
-        scratch_shapes=[V(o.shape, o.dtype) for o in shapes] + [D((2, 5))],
+        scratch_shapes=[D((5,))],
         name="hand_over",
-    )(*results)
+    )(*(pltpu.with_memory_space_constraint(r, V) for r in results))
     wgrad = jnp.swapaxes(wgrad.reshape(3, 3, 3, ch // nz, ch), 3, 4)
     return decoded, grad_latent, wgrad, ngrad.reshape(ch), bgrad.reshape(ch)
 

time: 77.3 us -> 73.8 us (0.955)
  Pallas kernels: 76.5 us -> 73.1 us
    pallas_call x1, Pallas kernels: 74.1 us -> 71.9 us  [per_device(): pl.pallas_call(functools.partial(kernel, nx, ny, nz, latent.shape), out_s...]
    pallas_call x1, Pallas kernels: 2.38 us -> 1.18 us  [per_device(): pl.pallas_call(hand_over, out_shape=shapes, in_specs=[anywhere] * 5, out_...]
where the time goes in v4:
time: 73.8 us; the launch traced here: 73.7 us
  Pallas kernels  73.1 us (99%)
    pallas_call x1, Pallas kernels, per_device(): pl.pallas_call(functools.partial(kernel, nx, ny, nz, latent.shape), out_s...  71.9 us

profile of v4, /device:TPU:1, one launch (start us, length us, event | category | flops | bytes accessed | tf_op | source)
XLA Modules:
  0.0 73.7 jit_solution(10066370492594332103)
XLA Ops:
  0.6 71.9 %block.1 = (bf16[2,4,80,256]{3,2,1,0:T(8,128)(2,1)S(1)}, bf16[2,4,80,256]{3,2,1,0:T(8,128)(2,1)S(1)}, f32[9,3,32,256]{3,2,1,0:T(8,128)S(1)}, f32[1,256]{1,0:T(1,128)S(1)}, f32[1,256]{1,0:T(1,128)S(1)}) custom-call(bf16[2,4,80,256]{3,2,1,0:T(8,128)(2,1)} %latent_hbm.1, bf16[2,4,80,256]{3,2,1,0:T(8,128)(2,1)} %target_hbm.1, bf16[9,768,256]{2,1,0:T(8,128)(2,1)} %bitcast.8, ...), custom_call_target="tpu_custom_call" | custom-call | tf_op jit(solution)/shard_map/block/pallas_call | solution.py:668
  72.5 1.2 %hand_over.1 = (bf16[2,4,80,256]{3,2,1,0:T(8,128)(2,1)}, bf16[2,4,80,256]{3,2,1,0:T(8,128)(2,1)}, f32[9,3,32,256]{3,2,1,0:T(8,128)}, f32[1,256]{1,0:T(1,128)}, f32[1,256]{1,0:T(1,128)}) custom-call(bf16[2,4,80,256]{3,2,1,0:T(8,128)(2,1)S(1)} %get-tuple-element.15.refs_0_, bf16[2,4,80,256]{3,2,1,0:T(8,128)(2,1)S(1)} %get-tuple-element.16.refs_1_, ...), custom_call_target="tpu_custom_call" | custom-call | tf_op jit(solution)/shard_map/hand_over/pallas_call | solution.py:690
